TPU v7x, 32 devices: a whole 2x2x4 slice. The times are simulated.
32 devices in a mesh: kv: 4 (over y, x), seq: 8 (over z, core).
Axes of the slice: x: 2, y: 2, z: 4, core: 2. Of those that a mesh axis runs over, the one named last changes fastest.
Arguments:
- sampled_rows: int32 [768], replicated, may hold values from 0 to 2047, as said below
- query_vectors: bfloat16 [768, 64, 128], P('seq', 'kv'), may hold values from -150 to 150
- key_vectors: bfloat16 [2048, 8, 128], P('seq', 'kv'), may hold values from -6 to 6
Outputs:
- heavy_hitters: float32 [2048], P('seq')
Inputs may be any that keep to these rules, and one draw needn't show every extreme that they name: `sampled_rows`: strictly increasing sequence positions.
All inputs are finite; a program needn't handle non-finite values.
Results may differ from a plain program's by a relative error of at most 0.0003.
Values may be sent and summed in bfloat16 or wider, within the bound.
No kernel may reach another device: no remote copies, remote signals or barrier semaphores. Data moves between devices by JAX's collectives and lax.ppermute only.
A program may use at most 64 MiB of HBM per device.

v0:
```python
import functools
import math

import jax
import jax.numpy as jnp
from jax import lax
from jax.experimental import pallas as pl
from jax.experimental.pallas import tpu as pltpu
from jax.sharding import PartitionSpec as P


NEG = -1e30
LOW = -1e20
SPAN = 2048
LANES = 256
CHUNK = 256
CONTRACT_LAST = (((1,), (1,)), ((), ()))
CONTRACT_INNER = (((1,), (0,)), ((), ()))
WHOLE = pl.BlockSpec(memory_space=pltpu.VMEM)
SCALARS = pl.BlockSpec(memory_space=pltpu.SMEM)


def grant(mebibytes):
    return pltpu.CompilerParams(vmem_limit_bytes=mebibytes << 20)


def round_up(value, step):
    return -(-value // step) * step


def prepare_kernel(offsets, row_ref, query_ref, mask_ref, turned_ref):
    rows, heads, depth = query_ref.shape
    groups, _, width = turned_ref.shape
    size = heads // groups
    extra = mask_ref.shape[1]
    block = mask_ref.shape[0] // offsets.shape[0]
    column = lax.broadcasted_iota(jnp.int32, (block, extra), 1)
    place = lax.broadcasted_iota(jnp.int32, (block, extra), 0)
    position = row_ref[...]

    def mask(index):
        hidden = (place + offsets[index] > position) & (column < rows)
        value = jnp.where(hidden, NEG, 0.0)
        mask_ref[pl.ds(pl.multiple_of(index * block, block), block), :] = value.astype(mask_ref.dtype)

    pl.loop(0, offsets.shape[0])(mask)
    wide = query_ref[...].astype(jnp.float32)
    eye = (
        lax.broadcasted_iota(jnp.int32, (depth, depth), 0)
        == lax.broadcasted_iota(jnp.int32, (depth, depth), 1)
    )
    eye = jnp.where(eye, 1.0, 0.0).astype(jnp.bfloat16)
    owner = lax.broadcasted_iota(jnp.int32, (extra, width), 1) // size
    hot = owner == lax.broadcasted_iota(jnp.int32, (extra, width), 0)
    hot = jnp.where(hot, 1.0, 0.0).astype(jnp.bfloat16)
    for g in range(groups):
        part = wide[:, g * size : (g + 1) * size, :].reshape(width, depth).astype(jnp.bfloat16)
        turned = lax.dot_general(eye, part, CONTRACT_LAST, preferred_element_type=jnp.float32)
        turned_ref[g, :depth, :] = turned.astype(turned_ref.dtype)
        turned_ref[g, depth:, :] = hot


def split_keys(key_refs, counts, keys, plain):
    groups = keys.shape[0]
    block = plain.shape[0] // groups

    def split(ref, index, first):
        plain[...] = ref[pl.ds(index * groups * block, groups * block), :].astype(jnp.float32)
        for g in range(groups):
            part = plain[pl.ds(g, block, stride=groups), :]
            keys[g, pl.ds(first, block), :] = part.astype(keys.dtype)

    done = 0
    for ref, count in zip(key_refs, counts, strict=True):
        if count == 1:
            split(ref, 0, done * block)
        else:

            @pl.loop(0, count)
            def _(i, ref=ref, done=done):
                split(ref, i, pl.multiple_of((done + i) * block, block))

        done += count


def tile_of(step, width):
    across = width // LANES
    first = (step % across) * LANES
    return step // across, pl.ds(pl.multiple_of(first, LANES), LANES)


def raw_scores(keys, mask_ref, turned_ref, step, here, base, held, top):
    g, lanes = tile_of(step, turned_ref.shape[2])
    shown = pl.ds(here.start + base, here.size)
    left = jnp.concatenate([keys[g, here, :], mask_ref[shown, :]], axis=1)
    value = lax.dot_general(
        left, turned_ref[g, :, lanes], CONTRACT_INNER, preferred_element_type=jnp.float32
    )
    held[here, :] = value
    return jnp.maximum(top, jnp.max(value.reshape(here.size // 8, 8, LANES), axis=0))


def stage_kernel(base, mask_ref, turned_ref, *refs):
    *key_refs, term_ref, top_ref, sum_ref, keys, plain, held = refs
    amount, depth = keys.shape[1:]
    width = turned_ref.shape[2]
    chunk = math.gcd(amount, CHUNK)
    factor = math.log2(math.e) / math.sqrt(depth)
    split_keys(key_refs, [1] * len(key_refs), keys, plain)

    @pl.loop(0, keys.shape[0] * (width // LANES))
    def _(step):
        columns = pl.ds(pl.multiple_of(step * LANES, LANES), LANES)
        top = jnp.full((8, LANES), LOW, jnp.float32)
        for b in range(amount // chunk):
            here = pl.ds(b * chunk, chunk)
            top = raw_scores(keys, mask_ref, turned_ref, step, here, base, held, top)
        top = jnp.max(top, axis=0, keepdims=True)
        summed = jnp.zeros((8, LANES), jnp.float32)
        for b in range(amount // chunk):
            here = pl.ds(b * chunk, chunk)
            value = jnp.exp2((held[here, :] - top) * factor)
            term_ref[here, columns] = value
            summed = summed + jnp.sum(value.reshape(chunk // 8, 8, LANES), axis=0)
        top_ref[:, columns] = top
        sum_ref[:, columns] = jnp.sum(summed, axis=0, keepdims=True)


def column_kernel(counts, copies, rows, early, offsets, mask_ref, turned_ref, *refs):
    stages = [refs[3 * i : 3 * i + 3] for i in range(early)]
    refs = refs[3 * early :]
    key_refs, (out_ref, keys, plain, total, *scores) = refs[: len(counts)], refs[len(counts) :]
    groups, amount, depth = keys.shape
    width = turned_ref.shape[2]
    block = plain.shape[0] // groups
    chunk = math.gcd(amount, CHUNK)
    factor = math.log2(math.e) / math.sqrt(depth)
    every = total.shape[0]
    base = every - amount
    split_keys(key_refs, counts, keys, plain)
    tiles = groups * (width // LANES)

    def score(step, here, held, top):
        return raw_scores(keys, mask_ref, turned_ref, step, here, base, held, top)

    def term(here, held, top, summed):
        value = jnp.exp2((held[here, :] - top) * factor)
        held[here, :] = value
        return summed + jnp.sum(value.reshape(here.size // 8, 8, LANES), axis=0)

    def spread(value, weight, there, first):
        value = value * weight
        part = value[:, :128]
        for i in range(1, LANES // 128):
            part = part + value[:, i * 128 : (i + 1) * 128]
        total[there, :] = part if first else total[there, :] + part

    lowest = jnp.full((8, LANES), LOW, jnp.float32)
    nothing = jnp.zeros((8, LANES), jnp.float32)
    if amount <= SPAN:
        top, weights = {}, {}
        parts = amount // chunk
        for step in range(tiles + 2):
            high, summed = lowest, nothing
            old = step - 2
            for b in range(parts):
                here = pl.ds(b * chunk, chunk)
                if 0 <= old:
                    first = 0
                    columns = pl.ds(old * LANES, LANES)
                    for (terms, _, _), weight in zip(stages, weights[old][1:], strict=True):
                        size = terms.shape[0] // parts
                        value = terms[pl.ds(b * size, size), columns]
                        spread(value, weight, pl.ds(first + b * size, size), old == 0)
                        first += terms.shape[0]
                    value = scores[old % 3][here, :]
                    spread(value, weights[old][0], pl.ds(base + b * chunk, chunk), old == 0)
                if 0 <= step - 1 < tiles:
                    summed = term(here, scores[(step - 1) % 3], top[step - 1], summed)
                if step < tiles:
                    high = score(step, here, scores[step % 3], high)
            if 0 <= step - 1 < tiles:
                columns = pl.ds((step - 1) * LANES, LANES)
                whole = jnp.sum(summed, axis=0, keepdims=True)
                scale = [jnp.exp2((s[1][:, columns] - top[step - 1]) * factor) for s in stages]
                for s, by in zip(stages, scale, strict=True):
                    whole = whole + s[2][:, columns] * by
                share = 1.0 / whole
                weights[step - 1] = [share] + [share * by for by in scale]
            if step < tiles:
                columns = pl.ds(step * LANES, LANES)
                peak = jnp.max(high, axis=0, keepdims=True)
                for s in stages:
                    peak = jnp.maximum(peak, s[1][:, columns])
                top[step] = peak
    else:
        total[...] = jnp.zeros_like(total)

        def over(body, carry):
            def at(i, c):
                return body(pl.ds(pl.multiple_of(i * chunk, chunk), chunk), c)

            return lax.fori_loop(0, amount // chunk, at, carry)

        @pl.loop(0, tiles)
        def _(step):
            held = scores[0]
            high = over(lambda here, c: score(step, here, held, c), lowest)
            peak = jnp.max(high, axis=0, keepdims=True)
            summed = over(lambda here, c: term(here, held, peak, c), nothing)
            share = 1.0 / jnp.sum(summed, axis=0, keepdims=True)

            def last(here, c):
                spread(held[here, :], share, here, False)
                return c

            over(last, 0)

    ones = jnp.ones((16, 128), jnp.bfloat16)

    def finish(index):
        here = pl.ds(pl.multiple_of(index * block, block), block)
        high = total[here, :].astype(jnp.bfloat16)
        low = (total[here, :] - high.astype(jnp.float32)).astype(jnp.bfloat16)
        line = sum(
            lax.dot_general(ones, part, CONTRACT_LAST, preferred_element_type=jnp.float32)
            for part in (high, low)
        )[:1]
        row = offsets[index] // block
        line = line * (1.0 / (width // rows))
        for i in range(copies):
            out_ref[i * (every // block) + row, :, :] = line

    if amount <= SPAN:
        for index in range(every // block):
            finish(index)
    else:
        pl.loop(0, every // block)(finish)


def gather_keys(key_vectors):
    size = lax.axis_size("seq")
    swap = [(i, i ^ 1) for i in range(size)]
    slots = {0: key_vectors}
    far = [4, 6, 2] if size == 8 else list(range(2, size, 2))
    for j in far:
        slots[j] = lax.ppermute(key_vectors, "seq", [(i, i ^ j) for i in range(size)])
    for j in [0] + far:
        slots[j + 1] = lax.ppermute(slots[j], "seq", swap)
    return slots, [i for j in [0] + far for i in (j, j + 1)]


def on_device(sampled_rows, query_vectors, key_vectors):
    local_rows, heads, depth = query_vectors.shape
    local_keys, groups, _ = key_vectors.shape
    width = local_rows * heads // groups
    members = lax.axis_size("seq")
    others = lax.axis_size("kv")
    me = lax.axis_index("seq")
    amount = members * local_keys
    extra = round_up(local_rows, 128)
    direct = members & (members - 1) == 0 and 2 < members <= 8
    if direct:
        slots, order = gather_keys(key_vectors)
        early = [order[i : i + 2] for i in range(0, members - 4, 2)]
        blocks = [slots[j] for j in order]
        counts = [1] * 4
        owner = me ^ jnp.array(order, jnp.int32)
    else:
        early = []
        blocks = [lax.all_gather(key_vectors, "seq", axis=0, tiled=True)]
        counts = [members]
        owner = jnp.arange(members, dtype=jnp.int32)
    blocks = [b.reshape(-1, depth) for b in blocks]
    offsets = owner * local_keys
    own_rows = lax.dynamic_slice_in_dim(sampled_rows, me * local_rows, local_rows, 0)
    own_rows = jnp.pad(own_rows, (0, extra - local_rows))[None, :]
    mask, turned = pl.pallas_call(
        prepare_kernel,
        out_shape=(
            jax.ShapeDtypeStruct((amount, extra), jnp.bfloat16),
            jax.ShapeDtypeStruct((groups, depth + extra, width), jnp.bfloat16),
        ),
        in_specs=[SCALARS, WHOLE, WHOLE],
        out_specs=(WHOLE, WHOLE),
        compiler_params=grant(8 if amount <= SPAN else 32),
        name="prepare",
    )(offsets, own_rows, query_vectors)
    stages = []
    for i, chosen in enumerate(early):
        some = len(chosen) * local_keys
        stages += pl.pallas_call(
            functools.partial(stage_kernel, i * some),
            out_shape=(
                jax.ShapeDtypeStruct((some, groups * width), jnp.float32),
                jax.ShapeDtypeStruct((1, groups * width), jnp.float32),
                jax.ShapeDtypeStruct((1, groups * width), jnp.float32),
            ),
            in_specs=[WHOLE] * (2 + len(chosen)),
            out_specs=(WHOLE,) * 3,
            scratch_shapes=[
                pltpu.VMEM((groups, some, depth), jnp.bfloat16),
                pltpu.VMEM((groups * local_keys, depth), jnp.float32),
                pltpu.VMEM((some, LANES), jnp.float32),
            ],
            compiler_params=grant(12),
        )(mask, turned, *blocks[2 * i : 2 * i + 2])
    blocks = blocks[2 * len(early) :]
    left = sum(counts) * local_keys
    partial = pl.pallas_call(
        functools.partial(column_kernel, counts, others, local_rows, len(early)),
        out_shape=jax.ShapeDtypeStruct((others * members, 1, local_keys), jnp.float32),
        in_specs=[SCALARS] + [WHOLE] * (2 + len(stages) + len(blocks)),
        out_specs=WHOLE,
        scratch_shapes=[
            pltpu.VMEM((groups, left, depth), jnp.bfloat16),
            pltpu.VMEM((groups * local_keys, depth), jnp.float32),
            pltpu.VMEM((amount, 128), jnp.float32),
        ]
        + [pltpu.VMEM((left, LANES), jnp.float32)] * (3 if left <= SPAN else 1),
        compiler_params=grant(24 if left <= SPAN else 60),
        name="columns",
    )(offsets, mask, turned, *stages, *blocks)
    received = lax.all_to_all(partial, ("kv", "seq"), 0, 0, tiled=True)
    return jnp.sum(received, axis=(0, 1))


def solution(mesh):
    placed = (P(), P("seq", "kv", None), P("seq", "kv", None))
    return jax.shard_map(on_device, mesh=mesh, in_specs=placed, out_specs=P("seq"), check_vma=False)
```

profile of v0, /device:TPU:0, one launch (start us, length us, event | category | flops | bytes accessed | tf_op | source)
XLA Modules:
  0.0 41.9 jit_solution(4892659136596872253)
XLA Ops:
  0.0 4.1 %collective-permute-start.1 = (bf16[256,2,128]{2,1,0:T(2,128)(2,1)}, bf16[256,2,128]{2,1,0:T(2,128)(2,1)S(1)}, u32[]{:S(2)}, u32[]{:S(2)}) collective-permute-start(bf16[256,2,128]{2,1,0:T(2,128)(2,1)} %param.6), channel_id=1, source_target_pairs={{0,4},{1,5},{2,6},{3,7},{4,0},{5,1},{6,2},{7,3},{8,12},{9,13},{10,... | collective-permute-start | bytes 393224 | tf_op jit(solution)/shard_map/ppermute | solution.py:247
  4.1 1.3 %collective-permute-start.3 = (bf16[256,2,128]{2,1,0:T(2,128)(2,1)}, bf16[256,2,128]{2,1,0:T(2,128)(2,1)S(1)}, u32[]{:S(2)}, u32[]{:S(2)}) collective-permute-start(bf16[256,2,128]{2,1,0:T(2,128)(2,1)} %param.6), channel_id=1, source_target_pairs={{0,6},{1,7},{2,4},{3,5},{4,2},{5,3},{6,0},{7,1},{8,14},{9,15},{10,... | collective-permute-start | bytes 393224 | tf_op jit(solution)/shard_map/ppermute | solution.py:247
  5.4 0.2 collective-permute-start.5
  5.6 0.0 collective-permute-start
  5.6 8.6 %collective-permute-done.1 = bf16[256,2,128]{2,1,0:T(2,128)(2,1)S(1)} collective-permute-done((bf16[256,2,128]{2,1,0:T(2,128)(2,1)}, bf16[256,2,128]{2,1,0:T(2,128)(2,1)S(1)}, u32[]{:S(2)}, u32[]{:S(2)}) %collective-permute-start.1) | collective-permute-done | bytes 131104 | tf_op jit(solution)/shard_map/ppermute | solution.py:247
  14.3 0.0 collective-permute-start.2
  14.3 0.0 collective-permute-done.3
  14.3 0.5 %collective-permute-start.4 = (bf16[256,2,128]{2,1,0:T(2,128)(2,1)S(1)}, bf16[256,2,128]{2,1,0:T(2,128)(2,1)S(1)}, u32[]{:S(2)}, u32[]{:S(2)}) collective-permute-start(bf16[256,2,128]{2,1,0:T(2,128)(2,1)S(1)} %collective-permute-done.3), channel_id=1, source_target_pairs={{0,1},{1,0},{2,3},{3,2},{4,5},{5,4},{6,7},{7,6},{8,9},{9,8},{10,11... | collective-permute-start | bytes 393224 | tf_op jit(solution)/shard_map/ppermute | solution.py:249
  14.8 0.0 collective-permute-done.5
  14.8 0.1 collective-permute-start.6
  14.9 0.7 %xor_multiply_fusion.offsets = s32[8]{0:T(128)S(1)} fusion(s32[8]{0:T(128)} %constant.16.clone, s32[]{:T(128)S(6)} %axis_index.12), kind=kLoop, calls=%fused_computation.1 | loop fusion | flops 16 | bytes 68 | tf_op jit(solution)/shard_map/mul | solution.py:275
  15.5 0.8 %dynamic_slice.3 = s32[96]{0:T(128)S(1)} dynamic-slice(s32[768]{0:T(1024)} %param.4, s32[]{:T(128)S(6)} %select_n.3), dynamic_slice_sizes={96} | dynamic-slice | bytes 772 | tf_op jit(solution)/shard_map/dynamic_slice | solution.py:276
  16.3 1.0 %copy-done = bf16[96,16,128]{2,1,0:T(8,128)(2,1)S(1)} copy-done((bf16[96,16,128]{2,1,0:T(8,128)(2,1)S(1)}, bf16[96,16,128]{2,1,0:T(8,128)(2,1)}, u32[]{:S(2)}) %copy-start) | copy-done | bytes 393240
  17.3 1.0 %prepare.1 = (bf16[2048,128]{1,0:T(8,128)(2,1)S(1)}, bf16[2,256,768]{2,1,0:T(8,128)(2,1)S(1)}) custom-call(s32[8]{0:T(128)S(1)} %xor_multiply_fusion.offsets, s32[1,128]{1,0:T(1,128)S(1)} %pad_bitcast_fusion.row_ref, bf16[96,16,128]{2,1,0:T(8,128)(2,1)S(1)} %copy-done), custom_call_target="tpu_custom_call" | custom-call | tf_op jit(solution)/shard_map/prepare/pallas_call | solution.py:278
  18.3 0.0 collective-permute-done
  18.3 0.0 copy-start.1
  18.3 0.9 %copy-done.1 = bf16[256,2,128]{2,1,0:T(2,128)(2,1)S(1)} copy-done((bf16[256,2,128]{2,1,0:T(2,128)(2,1)S(1)}, bf16[256,2,128]{2,1,0:T(2,128)(2,1)}, u32[]{:S(2)}) %copy-start.1) | copy-done | bytes 131096
  19.2 2.2 %shard_map.46 = (f32[512,1536]{1,0:T(8,128)S(1)}, f32[1,1536]{1,0:T(1,128)S(1)}, f32[1,1536]{1,0:T(1,128)S(1)}) custom-call(bf16[2048,128]{1,0:T(8,128)(2,1)S(1)} %get-tuple-element.13.mask_ref, bf16[2,256,768]{2,1,0:T(8,128)(2,1)S(1)} %get-tuple-element.14.turned_ref, bf16[512,128]{1,0:T(8,128)(2,1)S(1)} %bitcast.14, bf16[512,128]{1,0:T(8,128)(2,1)S(1)} %bitcast.16), custom_call_target="tpu_custom_call" | custom-call | tf_op jit(solution)/shard_map/pallas_call | solution.py:292
  21.4 0.0 collective-permute-done.2
  21.4 2.2 %shard_map.47 = (f32[512,1536]{1,0:T(8,128)S(1)}, f32[1,1536]{1,0:T(1,128)S(1)}, f32[1,1536]{1,0:T(1,128)S(1)}) custom-call(bf16[2048,128]{1,0:T(8,128)(2,1)S(1)} %get-tuple-element.13.mask_ref, bf16[2,256,768]{2,1,0:T(8,128)(2,1)S(1)} %get-tuple-element.14.turned_ref, bf16[512,128]{1,0:T(8,128)(2,1)S(1)} %bitcast.15, bf16[512,128]{1,0:T(8,128)(2,1)S(1)} %bitcast.17), custom_call_target="tpu_custom_call" | custom-call | tf_op jit(solution)/shard_map/pallas_call | solution.py:292
  23.6 0.0 collective-permute-done.4
  23.6 3.9 %columns.1 = f32[32,1,256]{2,1,0:T(1,128)S(1)} custom-call(s32[8]{0:T(128)S(1)} %xor_multiply_fusion.offsets, bf16[2048,128]{1,0:T(8,128)(2,1)S(1)} %get-tuple-element.13.mask_ref, bf16[2,256,768]{2,1,0:T(8,128)(2,1)S(1)} %get-tuple-element.14.turned_ref, f32[512,1536]{1,0:T(8,128)S(1)} %get-tuple-element.15.refs_0_, ...), custom_call_target="tpu_custom_call" | custom-call | tf_op jit(solution)/shard_map/columns/pallas_call | solution.py:310
  27.5 13.8 %all_to_all.5 = f32[32,1,256]{2,1,0:T(1,128)S(1)} all-to-all(f32[32,1,256]{2,1,0:T(1,128)S(1)} %columns.1), channel_id=1, replica_groups=mesh['kv'=4,'seq'=8] {'kv','seq'}, dimensions={0} | all-to-all | bytes 65536 | tf_op jit(solution)/shard_map/all_to_all | solution.py:324
  41.3 0.6 %reduce_sum.9 = f32[256]{0:T(256)} reduce(f32[32,1,256]{2,1,0:T(1,128)S(1)} %all_to_all.5, f32[]{:T(128)} %constant.6.clone.1), dimensions={0,1}, to_apply=%region_0.1 | reduce | flops 7936 | bytes 33796 | tf_op jit(solution)/shard_map/reduce_sum | solution.py:325
  (3 shorter events, 0.0 us)
Async XLA Ops:
  0.0 14.3 %collective-permute-start.1 = (bf16[256,2,128]{2,1,0:T(2,128)(2,1)}, bf16[256,2,128]{2,1,0:T(2,128)(2,1)S(1)}, u32[]{:S(2)}, u32[]{:S(2)}) collective-permute-start(bf16[256,2,128]{2,1,0:T(2,128)(2,1)} %param.6), channel_id=1, source_target_pairs={{0,4},{1,5},{2,6},{3,7},{4,0},{5,1},{6,2},{7,3},{8,12},{9,13},{10,... | collective-permute-start | bytes 393224 | tf_op jit(solution)/shard_map/ppermute | solution.py:247
  4.1 10.2 %collective-permute-start.3 = (bf16[256,2,128]{2,1,0:T(2,128)(2,1)}, bf16[256,2,128]{2,1,0:T(2,128)(2,1)S(1)}, u32[]{:S(2)}, u32[]{:S(2)}) collective-permute-start(bf16[256,2,128]{2,1,0:T(2,128)(2,1)} %param.6), channel_id=1, source_target_pairs={{0,6},{1,7},{2,4},{3,5},{4,2},{5,3},{6,0},{7,1},{8,14},{9,15},{10,... | collective-permute-start | bytes 393224 | tf_op jit(solution)/shard_map/ppermute | solution.py:247
  5.4 9.4 %collective-permute-start.5 = (bf16[256,2,128]{2,1,0:T(2,128)(2,1)}, bf16[256,2,128]{2,1,0:T(2,128)(2,1)S(1)}, u32[]{:S(2)}, u32[]{:S(2)}) collective-permute-start(bf16[256,2,128]{2,1,0:T(2,128)(2,1)} %param.6), channel_id=1, source_target_pairs={{0,2},{1,3},{2,0},{3,1},{4,6},{5,7},{6,4},{7,5},{8,10},{9,11},{10,... | collective-permute-start | bytes 393224 | tf_op jit(solution)/shard_map/ppermute | solution.py:247
  5.6 12.6 %collective-permute-start = (bf16[256,2,128]{2,1,0:T(2,128)(2,1)}, bf16[256,2,128]{2,1,0:T(2,128)(2,1)S(1)}, u32[]{:S(2)}, u32[]{:S(2)}) collective-permute-start(bf16[256,2,128]{2,1,0:T(2,128)(2,1)} %param.6), channel_id=1, source_target_pairs={{0,1},{1,0},{2,3},{3,2},{4,5},{5,4},{6,7},{7,6},{8,9},{9,8},{10,11... | collective-permute-start | bytes 393224 | tf_op jit(solution)/shard_map/ppermute | solution.py:249
  14.3 7.1 %collective-permute-start.2 = (bf16[256,2,128]{2,1,0:T(2,128)(2,1)S(1)}, bf16[256,2,128]{2,1,0:T(2,128)(2,1)S(1)}, u32[]{:S(2)}, u32[]{:S(2)}) collective-permute-start(bf16[256,2,128]{2,1,0:T(2,128)(2,1)S(1)} %collective-permute-done.1), channel_id=1, source_target_pairs={{0,1},{1,0},{2,3},{3,2},{4,5},{5,4},{6,7},{7,6},{8,9},{9,8},{10,11... | collective-permute-start | bytes 393224 | tf_op jit(solution)/shard_map/ppermute | solution.py:249
  14.3 9.3 %collective-permute-start.4 = (bf16[256,2,128]{2,1,0:T(2,128)(2,1)S(1)}, bf16[256,2,128]{2,1,0:T(2,128)(2,1)S(1)}, u32[]{:S(2)}, u32[]{:S(2)}) collective-permute-start(bf16[256,2,128]{2,1,0:T(2,128)(2,1)S(1)} %collective-permute-done.3), channel_id=1, source_target_pairs={{0,1},{1,0},{2,3},{3,2},{4,5},{5,4},{6,7},{7,6},{8,9},{9,8},{10,11... | collective-permute-start | bytes 393224 | tf_op jit(solution)/shard_map/ppermute | solution.py:249
  14.8 8.8 %collective-permute-start.6 = (bf16[256,2,128]{2,1,0:T(2,128)(2,1)S(1)}, bf16[256,2,128]{2,1,0:T(2,128)(2,1)S(1)}, u32[]{:S(2)}, u32[]{:S(2)}) collective-permute-start(bf16[256,2,128]{2,1,0:T(2,128)(2,1)S(1)} %collective-permute-done.5), channel_id=1, source_target_pairs={{0,1},{1,0},{2,3},{3,2},{4,5},{5,4},{6,7},{7,6},{8,9},{9,8},{10,11... | collective-permute-start | bytes 393224 | tf_op jit(solution)/shard_map/ppermute | solution.py:249
  16.3 1.0 %copy-start = (bf16[96,16,128]{2,1,0:T(8,128)(2,1)S(1)}, bf16[96,16,128]{2,1,0:T(8,128)(2,1)}, u32[]{:S(2)}) copy-start(bf16[96,16,128]{2,1,0:T(8,128)(2,1)} %query_ref.1) | copy-start | bytes 1179652
  18.3 0.9 %copy-start.1 = (bf16[256,2,128]{2,1,0:T(2,128)(2,1)S(1)}, bf16[256,2,128]{2,1,0:T(2,128)(2,1)}, u32[]{:S(2)}) copy-start(bf16[256,2,128]{2,1,0:T(2,128)(2,1)} %param.6) | copy-start | bytes 393220
where the time goes:
time: 42.1 us; the launch traced here: 41.9 us
  blocking collectives  13.8 us (33%)
  Pallas kernels  9.23 us (22%)
  waiting for transfers between devices  8.65 us (21%)
  starting transfers between devices  6.23 us (15%)
  local copies, waits for them, and re-layouts  2.66 us (6%)
  other arithmetic  1.27 us (3%)
    all_to_all x1, blocking collectives, on_device(): received = lax.all_to_all(partial, ('kv', 'seq'), 0, 0, tiled=True)  13.8 us
    ppermute x3, waiting for transfers between devices, gather_keys(): lax.ppermute(key_vectors, 'seq', [(i, i ^ j) for i in range(size)])  8.64 us
    ppermute x3, starting transfers between devices, gather_keys(): lax.ppermute(key_vectors, 'seq', [(i, i ^ j) for i in range(size)])  5.64 us
    pallas_call x2, Pallas kernels, on_device(): pl.pallas_call(functools.partial(stage_kernel, i * some), out_shape=(jax....  4.37 us
    pallas_call x1, Pallas kernels, on_device(): pl.pallas_call(functools.partial(column_kernel, counts, others, local_row...  3.89 us
    unnamed x4, local copies, waits for them, and re-layouts  1.89 us
    pallas_call x1, Pallas kernels, on_device(): pl.pallas_call(prepare_kernel, out_shape=(jax.ShapeDtypeStruct((amount, e...  0.96 us
  transfers between devices with their start and end apart: 7, of which 1 were waited for; matrix products, arithmetic and copies ran while one was open for 3% of the time, Pallas kernels for 13%

commit v1 on v0

--- a/solution.py
+++ b/solution.py
@@ -17,7 +17,6 @@
 CONTRACT_LAST = (((1,), (1,)), ((), ()))
 CONTRACT_INNER = (((1,), (0,)), ((), ()))
 WHOLE = pl.BlockSpec(memory_space=pltpu.VMEM)
-SCALARS = pl.BlockSpec(memory_space=pltpu.SMEM)
 
 
 def grant(mebibytes):
@@ -28,22 +27,36 @@
     return -(-value // step) * step
 
 
-def prepare_kernel(offsets, row_ref, query_ref, mask_ref, turned_ref):
+def owner_of(index, members, away):
+    if away is None:
+        return index
+    return ((lax.axis_index("seq") + members + away[index // 2]) % members) ^ (index % 2)
+
+
+def prepare_kernel(members, away, row_ref, query_ref, mask_ref, turned_ref):
     rows, heads, depth = query_ref.shape
     groups, _, width = turned_ref.shape
     size = heads // groups
     extra = mask_ref.shape[1]
-    block = mask_ref.shape[0] // offsets.shape[0]
+    block = mask_ref.shape[0] // members
     column = lax.broadcasted_iota(jnp.int32, (block, extra), 1)
     place = lax.broadcasted_iota(jnp.int32, (block, extra), 0)
-    position = row_ref[...]
+    first = lax.axis_index("seq") * rows
+    back = lax.rem(row_ref.shape[1] - first, row_ref.shape[1])
+    position = pltpu.roll(row_ref[...], back, 1)[:, :extra]
 
     def mask(index):
-        hidden = (place + offsets[index] > position) & (column < rows)
+        hidden = (place + owner_of(index, members, away) * block > position) & (column < rows)
         value = jnp.where(hidden, NEG, 0.0)
-        mask_ref[pl.ds(pl.multiple_of(index * block, block), block), :] = value.astype(mask_ref.dtype)
-
-    pl.loop(0, offsets.shape[0])(mask)
+        here = index * block
+        here = here if away else pl.multiple_of(here, block)
+        mask_ref[pl.ds(here, block), :] = value.astype(mask_ref.dtype)
+
+    if away is None:
+        pl.loop(0, members)(mask)
+    else:
+        for index in range(members):
+            mask(index)
     wide = query_ref[...].astype(jnp.float32)
     eye = (
         lax.broadcasted_iota(jnp.int32, (depth, depth), 0)
@@ -101,32 +114,35 @@
 
 
 def stage_kernel(base, mask_ref, turned_ref, *refs):
-    *key_refs, term_ref, top_ref, sum_ref, keys, plain, held = refs
+    *key_refs, term_ref, top_ref, sum_ref, keys, plain, even, odd = refs
     amount, depth = keys.shape[1:]
     width = turned_ref.shape[2]
     chunk = math.gcd(amount, CHUNK)
     factor = math.log2(math.e) / math.sqrt(depth)
     split_keys(key_refs, [1] * len(key_refs), keys, plain)
-
-    @pl.loop(0, keys.shape[0] * (width // LANES))
-    def _(step):
-        columns = pl.ds(pl.multiple_of(step * LANES, LANES), LANES)
+    tiles = keys.shape[0] * (width // LANES)
+    tops = {}
+    for step in range(tiles + 1):
         top = jnp.full((8, LANES), LOW, jnp.float32)
+        summed = jnp.zeros((8, LANES), jnp.float32)
+        columns = pl.ds((step - 1) * LANES, LANES)
         for b in range(amount // chunk):
             here = pl.ds(b * chunk, chunk)
-            top = raw_scores(keys, mask_ref, turned_ref, step, here, base, held, top)
-        top = jnp.max(top, axis=0, keepdims=True)
-        summed = jnp.zeros((8, LANES), jnp.float32)
-        for b in range(amount // chunk):
-            here = pl.ds(b * chunk, chunk)
-            value = jnp.exp2((held[here, :] - top) * factor)
-            term_ref[here, columns] = value
-            summed = summed + jnp.sum(value.reshape(chunk // 8, 8, LANES), axis=0)
-        top_ref[:, columns] = top
-        sum_ref[:, columns] = jnp.sum(summed, axis=0, keepdims=True)
-
-
-def column_kernel(counts, copies, rows, early, offsets, mask_ref, turned_ref, *refs):
+            if step:
+                held = (even, odd)[(step - 1) % 2]
+                value = jnp.exp2((held[here, :] - tops[step - 1]) * factor)
+                term_ref[here, columns] = value
+                summed = summed + jnp.sum(value.reshape(chunk // 8, 8, LANES), axis=0)
+            if step < tiles:
+                held = (even, odd)[step % 2]
+                top = raw_scores(keys, mask_ref, turned_ref, step, here, base, held, top)
+        if step:
+            top_ref[:, columns] = tops[step - 1]
+            sum_ref[:, columns] = jnp.sum(summed, axis=0, keepdims=True)
+        tops[step] = jnp.max(top, axis=0, keepdims=True)
+
+
+def column_kernel(members, away, counts, copies, rows, early, mask_ref, turned_ref, *refs):
     stages = [refs[3 * i : 3 * i + 3] for i in range(early)]
     refs = refs[3 * early :]
     key_refs, (out_ref, keys, plain, total, *scores) = refs[: len(counts)], refs[len(counts) :]
@@ -226,7 +242,7 @@
             lax.dot_general(ones, part, CONTRACT_LAST, preferred_element_type=jnp.float32)
             for part in (high, low)
         )[:1]
-        row = offsets[index] // block
+        row = owner_of(index, members, away)
         line = line * (1.0 / (width // rows))
         for i in range(copies):
             out_ref[i * (every // block) + row, :, :] = line
@@ -241,13 +257,15 @@
 def gather_keys(key_vectors):
     size = lax.axis_size("seq")
     swap = [(i, i ^ 1) for i in range(size)]
-    slots = {0: key_vectors}
-    far = [4, 6, 2] if size == 8 else list(range(2, size, 2))
-    for j in far:
-        slots[j] = lax.ppermute(key_vectors, "seq", [(i, i ^ j) for i in range(size)])
-    for j in [0] + far:
-        slots[j + 1] = lax.ppermute(slots[j], "seq", swap)
-    return slots, [i for j in [0] + far for i in (j, j + 1)]
+    ahead = [(i, (i + 2) % size) for i in range(size)]
+    blocks = {"own": key_vectors}
+    blocks["left"] = lax.ppermute(key_vectors, "seq", ahead)
+    blocks["right"] = lax.ppermute(key_vectors, "seq", [(j, i) for i, j in ahead])
+    blocks["far"] = lax.ppermute(blocks["left"], "seq", ahead)
+    found = []
+    for block in blocks.values():
+        found += [block, lax.ppermute(block, "seq", swap)]
+    return found, (0, -2, 2, -4)
 
 
 def on_device(sampled_rows, query_vectors, key_vectors):
@@ -256,39 +274,29 @@
     width = local_rows * heads // groups
     members = lax.axis_size("seq")
     others = lax.axis_size("kv")
-    me = lax.axis_index("seq")
     amount = members * local_keys
     extra = round_up(local_rows, 128)
-    direct = members & (members - 1) == 0 and 2 < members <= 8
-    if direct:
-        slots, order = gather_keys(key_vectors)
-        early = [order[i : i + 2] for i in range(0, members - 4, 2)]
-        blocks = [slots[j] for j in order]
-        counts = [1] * 4
-        owner = me ^ jnp.array(order, jnp.int32)
+    if members == 8:
+        blocks, away = gather_keys(key_vectors)
+        early, counts = 2, [1] * 4
     else:
-        early = []
-        blocks = [lax.all_gather(key_vectors, "seq", axis=0, tiled=True)]
-        counts = [members]
-        owner = jnp.arange(members, dtype=jnp.int32)
+        blocks, away = [lax.all_gather(key_vectors, "seq", axis=0, tiled=True)], None
+        early, counts = 0, [members]
     blocks = [b.reshape(-1, depth) for b in blocks]
-    offsets = owner * local_keys
-    own_rows = lax.dynamic_slice_in_dim(sampled_rows, me * local_rows, local_rows, 0)
-    own_rows = jnp.pad(own_rows, (0, extra - local_rows))[None, :]
     mask, turned = pl.pallas_call(
-        prepare_kernel,
+        functools.partial(prepare_kernel, members, away),
         out_shape=(
             jax.ShapeDtypeStruct((amount, extra), jnp.bfloat16),
             jax.ShapeDtypeStruct((groups, depth + extra, width), jnp.bfloat16),
         ),
-        in_specs=[SCALARS, WHOLE, WHOLE],
+        in_specs=[WHOLE, WHOLE],
         out_specs=(WHOLE, WHOLE),
         compiler_params=grant(8 if amount <= SPAN else 32),
         name="prepare",
-    )(offsets, own_rows, query_vectors)
+    )(sampled_rows[None, :], query_vectors)
     stages = []
-    for i, chosen in enumerate(early):
-        some = len(chosen) * local_keys
+    some = 2 * local_keys
+    for i in range(early):
         stages += pl.pallas_call(
             functools.partial(stage_kernel, i * some),
             out_shape=(
@@ -296,21 +304,21 @@
                 jax.ShapeDtypeStruct((1, groups * width), jnp.float32),
                 jax.ShapeDtypeStruct((1, groups * width), jnp.float32),
             ),
-            in_specs=[WHOLE] * (2 + len(chosen)),
+            in_specs=[WHOLE] * 4,
             out_specs=(WHOLE,) * 3,
             scratch_shapes=[
                 pltpu.VMEM((groups, some, depth), jnp.bfloat16),
                 pltpu.VMEM((groups * local_keys, depth), jnp.float32),
-                pltpu.VMEM((some, LANES), jnp.float32),
-            ],
+            ]
+            + [pltpu.VMEM((some, LANES), jnp.float32)] * 2,
             compiler_params=grant(12),
         )(mask, turned, *blocks[2 * i : 2 * i + 2])
-    blocks = blocks[2 * len(early) :]
+    blocks = blocks[2 * early :]
     left = sum(counts) * local_keys
     partial = pl.pallas_call(
-        functools.partial(column_kernel, counts, others, local_rows, len(early)),
+        functools.partial(column_kernel, members, away, counts, others, local_rows, early),
         out_shape=jax.ShapeDtypeStruct((others * members, 1, local_keys), jnp.float32),
-        in_specs=[SCALARS] + [WHOLE] * (2 + len(stages) + len(blocks)),
+        in_specs=[WHOLE] * (2 + len(stages) + len(blocks)),
         out_specs=WHOLE,
         scratch_shapes=[
             pltpu.VMEM((groups, left, depth), jnp.bfloat16),
@@ -320,7 +328,7 @@
         + [pltpu.VMEM((left, LANES), jnp.float32)] * (3 if left <= SPAN else 1),
         compiler_params=grant(24 if left <= SPAN else 60),
         name="columns",
-    )(offsets, mask, turned, *stages, *blocks)
+    )(mask, turned, *stages, *blocks)
     received = lax.all_to_all(partial, ("kv", "seq"), 0, 0, tiled=True)
     return jnp.sum(received, axis=(0, 1))
 

time: 42.1 us -> 36.7 us (0.87)
  Pallas kernels: 9.23 us -> 5.71 us
  blocking collectives: 13.8 us -> 11.1 us
  waiting for transfers between devices: 8.65 us -> 10.8 us
  other arithmetic: 1.27 us -> 0.62 us
  starting transfers between devices: 6.23 us -> 5.6 us
    all_to_all x1, blocking collectives: 13.8 us -> 11.1 us  [on_device(): received = lax.all_to_all(partial, ('kv', 'seq'), 0, 0, tiled=True)]
    pallas_call x2, Pallas kernels: 4.37 us -> 2.16 us  [on_device(): pl.pallas_call(functools.partial(stage_kernel, i * some), out_shape=(jax....]
    ppermute x7, waiting for transfers between devices: 8.65 us -> 10.8 us  [the longest x1 5.37 us: gather_keys(): blocks['far'] = lax.ppermute(blocks['left'], 'seq', ahead)]
    pallas_call x2, Pallas kernels: 4.85 us -> 3.55 us  [the longest x1 3.24 us: on_device(): pl.pallas_call(functools.partial(column_kernel, members, away, counts, ot...]
    dynamic_slice x1 -> x0, local copies, waits for them, and re-layouts: 0.76 us -> none  [on_device(): lax.dynamic_slice_in_dim(sampled_rows, me * local_rows, local_rows, 0)]
    broadcast_in_dim x1, local copies, waits for them, and re-layouts: 0.01 us -> 0.69 us  [on_device(): sampled_rows[None, :]]
    mul x1 -> x0, other arithmetic: 0.66 us -> none  [on_device(): offsets = owner * local_keys]
    ppermute x7, starting transfers between devices: 6.23 us -> 5.6 us  [the longest x1 3.05 us: gather_keys(): blocks['left'] = lax.ppermute(key_vectors, 'seq', ahead)]
  transfers between devices with their start and end apart: 7 -> 7, of which waited for: 1 -> 3; matrix products, arithmetic and copies ran while one was open for 3% -> 2% of each run, Pallas kernels for 13% -> 7%
where the time goes in v1:
time: 36.7 us; the launch traced here: 36.5 us
  blocking collectives  11.1 us (30%)
  waiting for transfers between devices  10.8 us (29%)
  Pallas kernels  5.71 us (16%)
  starting transfers between devices  5.6 us (15%)
  local copies, waits for them, and re-layouts  2.58 us (7%)
  other arithmetic  0.62 us (2%)
    all_to_all x1, blocking collectives, on_device(): received = lax.all_to_all(partial, ('kv', 'seq'), 0, 0, tiled=True)  11.1 us
    ppermute x1, waiting for transfers between devices, gather_keys(): blocks['far'] = lax.ppermute(blocks['left'], 'seq', ahead)  5.37 us
    ppermute x1, waiting for transfers between devices, gather_keys(): blocks['left'] = lax.ppermute(key_vectors, 'seq', ahead)  4.55 us
    pallas_call x1, Pallas kernels, on_device(): pl.pallas_call(functools.partial(column_kernel, members, away, counts, ot...  3.24 us
    ppermute x1, starting transfers between devices, gather_keys(): blocks['left'] = lax.ppermute(key_vectors, 'seq', ahead)  3.05 us
    pallas_call x2, Pallas kernels, on_device(): pl.pallas_call(functools.partial(stage_kernel, i * some), out_shape=(jax....  2.16 us
    ppermute x1, starting transfers between devices, gather_keys(): lax.ppermute(key_vectors, 'seq', [(j, i) for i, j in ahead])  2.03 us
    unnamed x4, local copies, waits for them, and re-layouts  1.89 us
  transfers between devices with their start and end apart: 7, of which 3 were waited for; matrix products, arithmetic and copies ran while one was open for 2% of the time, Pallas kernels for 7%

profile of v1, /device:TPU:0, one launch (start us, length us, event | category | flops | bytes accessed | tf_op | source)
XLA Modules:
  0.0 36.5 jit_solution(4357200054263464992)
XLA Ops:
  0.0 3.1 %collective-permute-start.1 = (bf16[256,2,128]{2,1,0:T(2,128)(2,1)}, bf16[256,2,128]{2,1,0:T(2,128)(2,1)S(1)}, u32[]{:S(2)}, u32[]{:S(2)}) collective-permute-start(bf16[256,2,128]{2,1,0:T(2,128)(2,1)} %param.5), channel_id=1, source_target_pairs={{0,2},{1,3},{2,4},{3,5},{4,6},{5,7},{6,0},{7,1},{8,10},{9,11},{10,... | collective-permute-start | bytes 393224 | tf_op jit(solution)/shard_map/ppermute | solution.py:262
  3.1 2.0 %collective-permute-start.3 = (bf16[256,2,128]{2,1,0:T(2,128)(2,1)}, bf16[256,2,128]{2,1,0:T(2,128)(2,1)S(1)}, u32[]{:S(2)}, u32[]{:S(2)}) collective-permute-start(bf16[256,2,128]{2,1,0:T(2,128)(2,1)} %param.5), channel_id=1, source_target_pairs={{2,0},{3,1},{4,2},{5,3},{6,4},{7,5},{0,6},{1,7},{10,8},{11,9},{12,... | collective-permute-start | bytes 393224 | tf_op jit(solution)/shard_map/ppermute | solution.py:263
  5.1 4.6 %collective-permute-done.1 = bf16[256,2,128]{2,1,0:T(2,128)(2,1)S(1)} collective-permute-done((bf16[256,2,128]{2,1,0:T(2,128)(2,1)}, bf16[256,2,128]{2,1,0:T(2,128)(2,1)S(1)}, u32[]{:S(2)}, u32[]{:S(2)}) %collective-permute-start.1) | collective-permute-done | bytes 131104 | tf_op jit(solution)/shard_map/ppermute | solution.py:262
  9.6 0.0 collective-permute-start.5
  9.6 0.0 collective-permute-start
  9.6 0.5 %collective-permute-start.2 = (bf16[256,2,128]{2,1,0:T(2,128)(2,1)S(1)}, bf16[256,2,128]{2,1,0:T(2,128)(2,1)S(1)}, u32[]{:S(2)}, u32[]{:S(2)}) collective-permute-start(bf16[256,2,128]{2,1,0:T(2,128)(2,1)S(1)} %collective-permute-done.1), channel_id=1, source_target_pairs={{0,1},{1,0},{2,3},{3,2},{4,5},{5,4},{6,7},{7,6},{8,9},{9,8},{10,11... | collective-permute-start | bytes 393224 | tf_op jit(solution)/shard_map/ppermute | solution.py:267
  10.2 0.9 %collective-permute-done.3 = bf16[256,2,128]{2,1,0:T(2,128)(2,1)S(1)} collective-permute-done((bf16[256,2,128]{2,1,0:T(2,128)(2,1)}, bf16[256,2,128]{2,1,0:T(2,128)(2,1)S(1)}, u32[]{:S(2)}, u32[]{:S(2)}) %collective-permute-start.3) | collective-permute-done | bytes 131104 | tf_op jit(solution)/shard_map/ppermute | solution.py:263
  11.0 0.0 collective-permute-start.4
  11.0 5.4 %collective-permute-done.5 = bf16[256,2,128]{2,1,0:T(2,128)(2,1)S(1)} collective-permute-done((bf16[256,2,128]{2,1,0:T(2,128)(2,1)S(1)}, bf16[256,2,128]{2,1,0:T(2,128)(2,1)S(1)}, u32[]{:S(2)}, u32[]{:S(2)}) %collective-permute-start.5) | collective-permute-done | bytes 131104 | tf_op jit(solution)/shard_map/ppermute | solution.py:264
  16.4 0.0 collective-permute-start.6
  16.4 0.7 %broadcast_in_dim.3.row_ref = s32[1,768]{1,0:T(1,128)S(1)} reshape(s32[768]{0:T(1024)} %param.3) | data formatting | bytes 6144 | tf_op jit(solution)/shard_map/broadcast_in_dim | solution.py:296
  17.1 1.0 %copy-done = bf16[96,16,128]{2,1,0:T(8,128)(2,1)S(1)} copy-done((bf16[96,16,128]{2,1,0:T(8,128)(2,1)S(1)}, bf16[96,16,128]{2,1,0:T(8,128)(2,1)}, u32[]{:S(2)}) %copy-start) | copy-done | bytes 393240
  18.1 0.3 prepare.1
  18.4 0.0 collective-permute-done
  18.4 0.0 copy-start.1
  18.4 0.9 %copy-done.1 = bf16[256,2,128]{2,1,0:T(2,128)(2,1)S(1)} copy-done((bf16[256,2,128]{2,1,0:T(2,128)(2,1)S(1)}, bf16[256,2,128]{2,1,0:T(2,128)(2,1)}, u32[]{:S(2)}) %copy-start.1) | copy-done | bytes 131096
  19.3 1.1 %shard_map.37 = (f32[512,1536]{1,0:T(8,128)S(1)}, f32[1,1536]{1,0:T(1,128)S(1)}, f32[1,1536]{1,0:T(1,128)S(1)}) custom-call(bf16[2048,128]{1,0:T(8,128)(2,1)S(1)} %get-tuple-element.13.mask_ref, bf16[2,256,768]{2,1,0:T(8,128)(2,1)S(1)} %get-tuple-element.14.turned_ref, bf16[512,128]{1,0:T(8,128)(2,1)S(1)} %bitcast.12, bf16[512,128]{1,0:T(8,128)(2,1)S(1)} %bitcast.15), custom_call_target="tpu_custom_call" | custom-call | tf_op jit(solution)/shard_map/pallas_call | solution.py:300
  20.4 0.0 collective-permute-done.2
  20.4 1.1 %shard_map.38 = (f32[512,1536]{1,0:T(8,128)S(1)}, f32[1,1536]{1,0:T(1,128)S(1)}, f32[1,1536]{1,0:T(1,128)S(1)}) custom-call(bf16[2048,128]{1,0:T(8,128)(2,1)S(1)} %get-tuple-element.13.mask_ref, bf16[2,256,768]{2,1,0:T(8,128)(2,1)S(1)} %get-tuple-element.14.turned_ref, bf16[512,128]{1,0:T(8,128)(2,1)S(1)} %bitcast.13, bf16[512,128]{1,0:T(8,128)(2,1)S(1)} %bitcast.14), custom_call_target="tpu_custom_call" | custom-call | tf_op jit(solution)/shard_map/pallas_call | solution.py:300
  21.5 0.0 collective-permute-done.4
  21.5 0.0 collective-permute-done.6
  21.5 3.2 %columns.1 = f32[32,1,256]{2,1,0:T(1,128)S(1)} custom-call(bf16[2048,128]{1,0:T(8,128)(2,1)S(1)} %get-tuple-element.13.mask_ref, bf16[2,256,768]{2,1,0:T(8,128)(2,1)S(1)} %get-tuple-element.14.turned_ref, f32[512,1536]{1,0:T(8,128)S(1)} %get-tuple-element.15.refs_0_, f32[1,1536]{1,0:T(1,128)S(1)} %get-tuple-element.16.refs_1_, ...), custom_call_target="tpu_custom_call" | custom-call | tf_op jit(solution)/shard_map/columns/pallas_call | solution.py:318
  24.8 11.1 %all_to_all.5 = f32[32,1,256]{2,1,0:T(1,128)S(1)} all-to-all(f32[32,1,256]{2,1,0:T(1,128)S(1)} %columns.1), channel_id=1, replica_groups=mesh['kv'=4,'seq'=8] {'kv','seq'}, dimensions={0} | all-to-all | bytes 65536 | tf_op jit(solution)/shard_map/all_to_all | solution.py:332
  35.8 0.6 %reduce_sum.9 = f32[256]{0:T(256)} reduce(f32[32,1,256]{2,1,0:T(1,128)S(1)} %all_to_all.5, f32[]{:T(128)} %constant.0.clone.1), dimensions={0,1}, to_apply=%region_0.0 | reduce | flops 7936 | bytes 33796 | tf_op jit(solution)/shard_map/reduce_sum | solution.py:333
  (1 shorter events, 0.0 us)
Async XLA Ops:
  0.0 9.6 %collective-permute-start.1 = (bf16[256,2,128]{2,1,0:T(2,128)(2,1)}, bf16[256,2,128]{2,1,0:T(2,128)(2,1)S(1)}, u32[]{:S(2)}, u32[]{:S(2)}) collective-permute-start(bf16[256,2,128]{2,1,0:T(2,128)(2,1)} %param.5), channel_id=1, source_target_pairs={{0,2},{1,3},{2,4},{3,5},{4,6},{5,7},{6,0},{7,1},{8,10},{9,11},{10,... | collective-permute-start | bytes 393224 | tf_op jit(solution)/shard_map/ppermute | solution.py:262
  3.1 8.0 %collective-permute-start.3 = (bf16[256,2,128]{2,1,0:T(2,128)(2,1)}, bf16[256,2,128]{2,1,0:T(2,128)(2,1)S(1)}, u32[]{:S(2)}, u32[]{:S(2)}) collective-permute-start(bf16[256,2,128]{2,1,0:T(2,128)(2,1)} %param.5), channel_id=1, source_target_pairs={{2,0},{3,1},{4,2},{5,3},{6,4},{7,5},{0,6},{1,7},{10,8},{11,9},{12,... | collective-permute-start | bytes 393224 | tf_op jit(solution)/shard_map/ppermute | solution.py:263
  9.6 6.8 %collective-permute-start.5 = (bf16[256,2,128]{2,1,0:T(2,128)(2,1)S(1)}, bf16[256,2,128]{2,1,0:T(2,128)(2,1)S(1)}, u32[]{:S(2)}, u32[]{:S(2)}) collective-permute-start(bf16[256,2,128]{2,1,0:T(2,128)(2,1)S(1)} %collective-permute-done.1), channel_id=1, source_target_pairs={{0,2},{1,3},{2,4},{3,5},{4,6},{5,7},{6,0},{7,1},{8,10},{9,11},{10,... | collective-permute-start | bytes 393224 | tf_op jit(solution)/shard_map/ppermute | solution.py:264
  9.6 8.8 %collective-permute-start = (bf16[256,2,128]{2,1,0:T(2,128)(2,1)}, bf16[256,2,128]{2,1,0:T(2,128)(2,1)S(1)}, u32[]{:S(2)}, u32[]{:S(2)}) collective-permute-start(bf16[256,2,128]{2,1,0:T(2,128)(2,1)} %param.5), channel_id=1, source_target_pairs={{0,1},{1,0},{2,3},{3,2},{4,5},{5,4},{6,7},{7,6},{8,9},{9,8},{10,11... | collective-permute-start | bytes 393224 | tf_op jit(solution)/shard_map/ppermute | solution.py:267
  9.6 10.8 %collective-permute-start.2 = (bf16[256,2,128]{2,1,0:T(2,128)(2,1)S(1)}, bf16[256,2,128]{2,1,0:T(2,128)(2,1)S(1)}, u32[]{:S(2)}, u32[]{:S(2)}) collective-permute-start(bf16[256,2,128]{2,1,0:T(2,128)(2,1)S(1)} %collective-permute-done.1), channel_id=1, source_target_pairs={{0,1},{1,0},{2,3},{3,2},{4,5},{5,4},{6,7},{7,6},{8,9},{9,8},{10,11... | collective-permute-start | bytes 393224 | tf_op jit(solution)/shard_map/ppermute | solution.py:267
  11.0 10.5 %collective-permute-start.4 = (bf16[256,2,128]{2,1,0:T(2,128)(2,1)S(1)}, bf16[256,2,128]{2,1,0:T(2,128)(2,1)S(1)}, u32[]{:S(2)}, u32[]{:S(2)}) collective-permute-start(bf16[256,2,128]{2,1,0:T(2,128)(2,1)S(1)} %collective-permute-done.3), channel_id=1, source_target_pairs={{0,1},{1,0},{2,3},{3,2},{4,5},{5,4},{6,7},{7,6},{8,9},{9,8},{10,11... | collective-permute-start | bytes 393224 | tf_op jit(solution)/shard_map/ppermute | solution.py:267
  16.4 5.1 %collective-permute-start.6 = (bf16[256,2,128]{2,1,0:T(2,128)(2,1)S(1)}, bf16[256,2,128]{2,1,0:T(2,128)(2,1)S(1)}, u32[]{:S(2)}, u32[]{:S(2)}) collective-permute-start(bf16[256,2,128]{2,1,0:T(2,128)(2,1)S(1)} %collective-permute-done.5), channel_id=1, source_target_pairs={{0,1},{1,0},{2,3},{3,2},{4,5},{5,4},{6,7},{7,6},{8,9},{9,8},{10,11... | collective-permute-start | bytes 393224 | tf_op jit(solution)/shard_map/ppermute | solution.py:267
  17.1 1.0 %copy-start = (bf16[96,16,128]{2,1,0:T(8,128)(2,1)S(1)}, bf16[96,16,128]{2,1,0:T(8,128)(2,1)}, u32[]{:S(2)}) copy-start(bf16[96,16,128]{2,1,0:T(8,128)(2,1)} %query_ref.1) | copy-start | bytes 1179652
  18.4 0.9 %copy-start.1 = (bf16[256,2,128]{2,1,0:T(2,128)(2,1)S(1)}, bf16[256,2,128]{2,1,0:T(2,128)(2,1)}, u32[]{:S(2)}) copy-start(bf16[256,2,128]{2,1,0:T(2,128)(2,1)} %param.5) | copy-start | bytes 393220

commit v2 on v1

--- a/solution.py
+++ b/solution.py
@@ -17,6 +17,7 @@
 CONTRACT_LAST = (((1,), (1,)), ((), ()))
 CONTRACT_INNER = (((1,), (0,)), ((), ()))
 WHOLE = pl.BlockSpec(memory_space=pltpu.VMEM)
+ANYWHERE = pl.BlockSpec(memory_space=pltpu.HBM)
 
 
 def grant(mebibytes):
@@ -33,17 +34,22 @@
     return ((lax.axis_index("seq") + members + away[index // 2]) % members) ^ (index % 2)
 
 
-def prepare_kernel(members, away, row_ref, query_ref, mask_ref, turned_ref):
+def prepare_kernel(members, away, row_ref, query_hbm, key_hbm, mask_ref, turned_ref, key_ref, query_ref, sem):
     rows, heads, depth = query_ref.shape
     groups, _, width = turned_ref.shape
+    fetch_query = pltpu.make_async_copy(query_hbm, query_ref, sem.at[0])
+    fetch_key = pltpu.make_async_copy(key_hbm, key_ref, sem.at[1])
+    fetch_query.start()
+    fetch_key.start()
     size = heads // groups
     extra = mask_ref.shape[1]
     block = mask_ref.shape[0] // members
     column = lax.broadcasted_iota(jnp.int32, (block, extra), 1)
     place = lax.broadcasted_iota(jnp.int32, (block, extra), 0)
     first = lax.axis_index("seq") * rows
-    back = lax.rem(row_ref.shape[1] - first, row_ref.shape[1])
-    position = pltpu.roll(row_ref[...], back, 1)[:, :extra]
+    total = row_ref.shape[0]
+    back = lax.rem(total - first, total)
+    position = pltpu.roll(row_ref[...].reshape(1, total), back, 1)[:, :extra]
 
     def mask(index):
         hidden = (place + owner_of(index, members, away) * block > position) & (column < rows)
@@ -57,6 +63,7 @@
     else:
         for index in range(members):
             mask(index)
+    fetch_query.wait()
     wide = query_ref[...].astype(jnp.float32)
     eye = (
         lax.broadcasted_iota(jnp.int32, (depth, depth), 0)
@@ -71,6 +78,7 @@
         turned = lax.dot_general(eye, part, CONTRACT_LAST, preferred_element_type=jnp.float32)
         turned_ref[g, :depth, :] = turned.astype(turned_ref.dtype)
         turned_ref[g, depth:, :] = hot
+    fetch_key.wait()
 
 
 def split_keys(key_refs, counts, keys, plain):
@@ -278,22 +286,33 @@
     extra = round_up(local_rows, 128)
     if members == 8:
         blocks, away = gather_keys(key_vectors)
-        early, counts = 2, [1] * 4
+        early, counts = 3, [1] * 2
     else:
         blocks, away = [lax.all_gather(key_vectors, "seq", axis=0, tiled=True)], None
         early, counts = 0, [members]
     blocks = [b.reshape(-1, depth) for b in blocks]
-    mask, turned = pl.pallas_call(
+    mask, turned, own = pl.pallas_call(
         functools.partial(prepare_kernel, members, away),
         out_shape=(
             jax.ShapeDtypeStruct((amount, extra), jnp.bfloat16),
             jax.ShapeDtypeStruct((groups, depth + extra, width), jnp.bfloat16),
+            jax.ShapeDtypeStruct((local_keys * groups, depth), jnp.bfloat16),
         ),
-        in_specs=[WHOLE, WHOLE],
-        out_specs=(WHOLE, WHOLE),
+        in_specs=[WHOLE, ANYWHERE, ANYWHERE],
+        out_specs=(WHOLE, WHOLE, WHOLE),
+        scratch_shapes=[
+            pltpu.VMEM(query_vectors.shape, jnp.bfloat16),
+            pltpu.SemaphoreType.DMA((2,)),
+        ],
         compiler_params=grant(8 if amount <= SPAN else 32),
         name="prepare",
-    )(sampled_rows[None, :], query_vectors)
+    )(
+        sampled_rows,
+        pltpu.with_memory_space_constraint(query_vectors, pltpu.HBM),
+        pltpu.with_memory_space_constraint(key_vectors.reshape(-1, depth), pltpu.HBM),
+    )
+    if early:
+        blocks[0] = own
     stages = []
     some = 2 * local_keys
     for i in range(early):

time: 36.7 us -> 35.7 us (0.973)
  local copies, waits for them, and re-layouts: 2.58 us -> 0.69 us
  Pallas kernels: 5.71 us -> 6.72 us
    unnamed x4 -> x2, local copies, waits for them, and re-layouts: 1.89 us -> 0.69 us
    pallas_call x2 -> x3, Pallas kernels: 2.16 us -> 3.24 us  [on_device(): pl.pallas_call(functools.partial(stage_kernel, i * some), out_shape=(jax....]
    pallas_call x1, Pallas kernels: 3.24 us -> 2.17 us  [on_device(): pl.pallas_call(functools.partial(column_kernel, members, away, counts, ot...]
    pallas_call x1, Pallas kernels: 0.31 us -> 1.3 us  [on_device(): pl.pallas_call(functools.partial(prepare_kernel, members, away), out_shap...]
    broadcast_in_dim x1 -> x0, local copies, waits for them, and re-layouts: 0.69 us -> none  [on_device(): sampled_rows[None, :]]
  transfers between devices with their start and end apart: 7 -> 7, of which waited for: 3 -> 3; matrix products, arithmetic and copies ran while one was open for 2% -> 0% of each run, Pallas kernels for 7% -> 13%
where the time goes in v2:
time: 35.7 us; the launch traced here: 35.5 us
  blocking collectives  11.1 us (31%)
  waiting for transfers between devices  10.8 us (30%)
  Pallas kernels  6.72 us (19%)
  starting transfers between devices  5.6 us (16%)
  local copies, waits for them, and re-layouts  0.69 us (2%)
  other arithmetic  0.62 us (2%)
    all_to_all x1, blocking collectives, on_device(): received = lax.all_to_all(partial, ('kv', 'seq'), 0, 0, tiled=True)  11.1 us
    ppermute x1, waiting for transfers between devices, gather_keys(): blocks['far'] = lax.ppermute(blocks['left'], 'seq', ahead)  5.37 us
    ppermute x1, waiting for transfers between devices, gather_keys(): blocks['left'] = lax.ppermute(key_vectors, 'seq', ahead)  4.55 us
    pallas_call x3, Pallas kernels, on_device(): pl.pallas_call(functools.partial(stage_kernel, i * some), out_shape=(jax....  3.24 us
    ppermute x1, starting transfers between devices, gather_keys(): blocks['left'] = lax.ppermute(key_vectors, 'seq', ahead)  3.05 us
    pallas_call x1, Pallas kernels, on_device(): pl.pallas_call(functools.partial(column_kernel, members, away, counts, ot...  2.17 us
    ppermute x1, starting transfers between devices, gather_keys(): lax.ppermute(key_vectors, 'seq', [(j, i) for i, j in ahead])  2.03 us
    pallas_call x1, Pallas kernels, on_device(): pl.pallas_call(functools.partial(prepare_kernel, members, away), out_shap...  1.3 us
  transfers between devices with their start and end apart: 7, of which 3 were waited for; matrix products, arithmetic and copies ran while one was open for 0% of the time, Pallas kernels for 13%

profile of v2, /device:TPU:0, one launch (start us, length us, event | category | flops | bytes accessed | tf_op | source)
XLA Modules:
  0.0 35.5 jit_solution(15005285828542652602)
XLA Ops:
  0.0 3.1 %collective-permute-start.1 = (bf16[256,2,128]{2,1,0:T(2,128)(2,1)}, bf16[256,2,128]{2,1,0:T(2,128)(2,1)S(1)}, u32[]{:S(2)}, u32[]{:S(2)}) collective-permute-start(bf16[256,2,128]{2,1,0:T(2,128)(2,1)} %param.5), channel_id=1, source_target_pairs={{0,2},{1,3},{2,4},{3,5},{4,6},{5,7},{6,0},{7,1},{8,10},{9,11},{10,... | collective-permute-start | bytes 393224 | tf_op jit(solution)/shard_map/ppermute | solution.py:270
  3.1 2.0 %collective-permute-start.3 = (bf16[256,2,128]{2,1,0:T(2,128)(2,1)}, bf16[256,2,128]{2,1,0:T(2,128)(2,1)S(1)}, u32[]{:S(2)}, u32[]{:S(2)}) collective-permute-start(bf16[256,2,128]{2,1,0:T(2,128)(2,1)} %param.5), channel_id=1, source_target_pairs={{2,0},{3,1},{4,2},{5,3},{6,4},{7,5},{0,6},{1,7},{10,8},{11,9},{12,... | collective-permute-start | bytes 393224 | tf_op jit(solution)/shard_map/ppermute | solution.py:271
  5.1 4.6 %collective-permute-done.1 = bf16[256,2,128]{2,1,0:T(2,128)(2,1)S(1)} collective-permute-done((bf16[256,2,128]{2,1,0:T(2,128)(2,1)}, bf16[256,2,128]{2,1,0:T(2,128)(2,1)S(1)}, u32[]{:S(2)}, u32[]{:S(2)}) %collective-permute-start.1) | collective-permute-done | bytes 131104 | tf_op jit(solution)/shard_map/ppermute | solution.py:270
  9.6 0.0 collective-permute-start.5
  9.6 0.0 collective-permute-start
  9.6 0.5 %collective-permute-start.2 = (bf16[256,2,128]{2,1,0:T(2,128)(2,1)S(1)}, bf16[256,2,128]{2,1,0:T(2,128)(2,1)S(1)}, u32[]{:S(2)}, u32[]{:S(2)}) collective-permute-start(bf16[256,2,128]{2,1,0:T(2,128)(2,1)S(1)} %collective-permute-done.1), channel_id=1, source_target_pairs={{0,1},{1,0},{2,3},{3,2},{4,5},{5,4},{6,7},{7,6},{8,9},{9,8},{10,11... | collective-permute-start | bytes 393224 | tf_op jit(solution)/shard_map/ppermute | solution.py:275
  10.2 0.9 %collective-permute-done.3 = bf16[256,2,128]{2,1,0:T(2,128)(2,1)S(1)} collective-permute-done((bf16[256,2,128]{2,1,0:T(2,128)(2,1)}, bf16[256,2,128]{2,1,0:T(2,128)(2,1)S(1)}, u32[]{:S(2)}, u32[]{:S(2)}) %collective-permute-start.3) | collective-permute-done | bytes 131104 | tf_op jit(solution)/shard_map/ppermute | solution.py:271
  11.0 0.0 collective-permute-start.4
  11.0 5.4 %collective-permute-done.5 = bf16[256,2,128]{2,1,0:T(2,128)(2,1)S(1)} collective-permute-done((bf16[256,2,128]{2,1,0:T(2,128)(2,1)S(1)}, bf16[256,2,128]{2,1,0:T(2,128)(2,1)S(1)}, u32[]{:S(2)}, u32[]{:S(2)}) %collective-permute-start.5) | collective-permute-done | bytes 131104 | tf_op jit(solution)/shard_map/ppermute | solution.py:272
  16.4 0.0 collective-permute-start.6
  16.4 0.0 copy-start
  16.4 0.7 %copy-done = s32[768]{0:T(1024)S(1)} copy-done((s32[768]{0:T(1024)S(1)}, s32[768]{0:T(1024)}, u32[]{:S(2)}) %copy-start) | copy-done | bytes 3096
  17.1 1.3 %prepare.1 = (bf16[2048,128]{1,0:T(8,128)(2,1)S(1)}, bf16[2,256,768]{2,1,0:T(8,128)(2,1)S(1)}, bf16[512,128]{1,0:T(8,128)(2,1)S(1)}) custom-call(s32[768]{0:T(1024)S(1)} %copy-done, bf16[96,16,128]{2,1,0:T(8,128)(2,1)} %query_hbm.1, bf16[512,128]{1,0:T(8,128)(2,1)} %bitcast.15), custom_call_target="tpu_custom_call" | custom-call | tf_op jit(solution)/shard_map/prepare/pallas_call | solution.py:294
  18.4 0.0 collective-permute-done
  18.4 1.1 %shard_map.37 = (f32[512,1536]{1,0:T(8,128)S(1)}, f32[1,1536]{1,0:T(1,128)S(1)}, f32[1,1536]{1,0:T(1,128)S(1)}) custom-call(bf16[2048,128]{1,0:T(8,128)(2,1)S(1)} %get-tuple-element.17.mask_ref, bf16[2,256,768]{2,1,0:T(8,128)(2,1)S(1)} %get-tuple-element.18.turned_ref, bf16[512,128]{1,0:T(8,128)(2,1)S(1)} %get-tuple-element.19.refs_0_, ...), custom_call_target="tpu_custom_call" | custom-call | tf_op jit(solution)/shard_map/pallas_call | solution.py:319
  19.5 0.0 collective-permute-done.2
  19.5 1.1 %shard_map.38 = (f32[512,1536]{1,0:T(8,128)S(1)}, f32[1,1536]{1,0:T(1,128)S(1)}, f32[1,1536]{1,0:T(1,128)S(1)}) custom-call(bf16[2048,128]{1,0:T(8,128)(2,1)S(1)} %get-tuple-element.17.mask_ref, bf16[2,256,768]{2,1,0:T(8,128)(2,1)S(1)} %get-tuple-element.18.turned_ref, bf16[512,128]{1,0:T(8,128)(2,1)S(1)} %bitcast.11, bf16[512,128]{1,0:T(8,128)(2,1)S(1)} %bitcast.13), custom_call_target="tpu_custom_call" | custom-call | tf_op jit(solution)/shard_map/pallas_call | solution.py:319
  20.6 0.0 collective-permute-done.4
  20.6 1.1 %shard_map.39 = (f32[512,1536]{1,0:T(8,128)S(1)}, f32[1,1536]{1,0:T(1,128)S(1)}, f32[1,1536]{1,0:T(1,128)S(1)}) custom-call(bf16[2048,128]{1,0:T(8,128)(2,1)S(1)} %get-tuple-element.17.mask_ref, bf16[2,256,768]{2,1,0:T(8,128)(2,1)S(1)} %get-tuple-element.18.turned_ref, bf16[512,128]{1,0:T(8,128)(2,1)S(1)} %bitcast.10, bf16[512,128]{1,0:T(8,128)(2,1)S(1)} %bitcast.12), custom_call_target="tpu_custom_call" | custom-call | tf_op jit(solution)/shard_map/pallas_call | solution.py:319
  21.7 0.0 collective-permute-done.6
  21.7 2.2 %columns.1 = f32[32,1,256]{2,1,0:T(1,128)S(1)} custom-call(bf16[2048,128]{1,0:T(8,128)(2,1)S(1)} %get-tuple-element.17.mask_ref, bf16[2,256,768]{2,1,0:T(8,128)(2,1)S(1)} %get-tuple-element.18.turned_ref, f32[512,1536]{1,0:T(8,128)S(1)} %get-tuple-element.20.refs_0_, f32[1,1536]{1,0:T(1,128)S(1)} %get-tuple-element.21.refs_1_, ...), custom_call_target="tpu_custom_call" | custom-call | tf_op jit(solution)/shard_map/columns/pallas_call | solution.py:337
  23.9 11.1 %all_to_all.5 = f32[32,1,256]{2,1,0:T(1,128)S(1)} all-to-all(f32[32,1,256]{2,1,0:T(1,128)S(1)} %columns.1), channel_id=1, replica_groups=mesh['kv'=4,'seq'=8] {'kv','seq'}, dimensions={0} | all-to-all | bytes 65536 | tf_op jit(solution)/shard_map/all_to_all | solution.py:351
  34.9 0.6 %reduce_sum.9 = f32[256]{0:T(256)} reduce(f32[32,1,256]{2,1,0:T(1,128)S(1)} %all_to_all.5, f32[]{:T(128)} %constant.0.clone.1), dimensions={0,1}, to_apply=%region_0.0 | reduce | flops 7936 | bytes 33796 | tf_op jit(solution)/shard_map/reduce_sum | solution.py:352
Async XLA Ops:
  0.0 9.6 %collective-permute-start.1 = (bf16[256,2,128]{2,1,0:T(2,128)(2,1)}, bf16[256,2,128]{2,1,0:T(2,128)(2,1)S(1)}, u32[]{:S(2)}, u32[]{:S(2)}) collective-permute-start(bf16[256,2,128]{2,1,0:T(2,128)(2,1)} %param.5), channel_id=1, source_target_pairs={{0,2},{1,3},{2,4},{3,5},{4,6},{5,7},{6,0},{7,1},{8,10},{9,11},{10,... | collective-permute-start | bytes 393224 | tf_op jit(solution)/shard_map/ppermute | solution.py:270
  3.1 8.0 %collective-permute-start.3 = (bf16[256,2,128]{2,1,0:T(2,128)(2,1)}, bf16[256,2,128]{2,1,0:T(2,128)(2,1)S(1)}, u32[]{:S(2)}, u32[]{:S(2)}) collective-permute-start(bf16[256,2,128]{2,1,0:T(2,128)(2,1)} %param.5), channel_id=1, source_target_pairs={{2,0},{3,1},{4,2},{5,3},{6,4},{7,5},{0,6},{1,7},{10,8},{11,9},{12,... | collective-permute-start | bytes 393224 | tf_op jit(solution)/shard_map/ppermute | solution.py:271
  9.6 6.8 %collective-permute-start.5 = (bf16[256,2,128]{2,1,0:T(2,128)(2,1)S(1)}, bf16[256,2,128]{2,1,0:T(2,128)(2,1)S(1)}, u32[]{:S(2)}, u32[]{:S(2)}) collective-permute-start(bf16[256,2,128]{2,1,0:T(2,128)(2,1)S(1)} %collective-permute-done.1), channel_id=1, source_target_pairs={{0,2},{1,3},{2,4},{3,5},{4,6},{5,7},{6,0},{7,1},{8,10},{9,11},{10,... | collective-permute-start | bytes 393224 | tf_op jit(solution)/shard_map/ppermute | solution.py:272
  9.6 8.8 %collective-permute-start = (bf16[256,2,128]{2,1,0:T(2,128)(2,1)}, bf16[256,2,128]{2,1,0:T(2,128)(2,1)S(1)}, u32[]{:S(2)}, u32[]{:S(2)}) collective-permute-start(bf16[256,2,128]{2,1,0:T(2,128)(2,1)} %param.5), channel_id=1, source_target_pairs={{0,1},{1,0},{2,3},{3,2},{4,5},{5,4},{6,7},{7,6},{8,9},{9,8},{10,11... | collective-permute-start | bytes 393224 | tf_op jit(solution)/shard_map/ppermute | solution.py:275
  9.6 9.9 %collective-permute-start.2 = (bf16[256,2,128]{2,1,0:T(2,128)(2,1)S(1)}, bf16[256,2,128]{2,1,0:T(2,128)(2,1)S(1)}, u32[]{:S(2)}, u32[]{:S(2)}) collective-permute-start(bf16[256,2,128]{2,1,0:T(2,128)(2,1)S(1)} %collective-permute-done.1), channel_id=1, source_target_pairs={{0,1},{1,0},{2,3},{3,2},{4,5},{5,4},{6,7},{7,6},{8,9},{9,8},{10,11... | collective-permute-start | bytes 393224 | tf_op jit(solution)/shard_map/ppermute | solution.py:275
  11.0 9.6 %collective-permute-start.4 = (bf16[256,2,128]{2,1,0:T(2,128)(2,1)S(1)}, bf16[256,2,128]{2,1,0:T(2,128)(2,1)S(1)}, u32[]{:S(2)}, u32[]{:S(2)}) collective-permute-start(bf16[256,2,128]{2,1,0:T(2,128)(2,1)S(1)} %collective-permute-done.3), channel_id=1, source_target_pairs={{0,1},{1,0},{2,3},{3,2},{4,5},{5,4},{6,7},{7,6},{8,9},{9,8},{10,11... | collective-permute-start | bytes 393224 | tf_op jit(solution)/shard_map/ppermute | solution.py:275
  16.4 5.3 %collective-permute-start.6 = (bf16[256,2,128]{2,1,0:T(2,128)(2,1)S(1)}, bf16[256,2,128]{2,1,0:T(2,128)(2,1)S(1)}, u32[]{:S(2)}, u32[]{:S(2)}) collective-permute-start(bf16[256,2,128]{2,1,0:T(2,128)(2,1)S(1)} %collective-permute-done.5), channel_id=1, source_target_pairs={{0,1},{1,0},{2,3},{3,2},{4,5},{5,4},{6,7},{7,6},{8,9},{9,8},{10,11... | collective-permute-start | bytes 393224 | tf_op jit(solution)/shard_map/ppermute | solution.py:275
  16.4 0.7 %copy-start = (s32[768]{0:T(1024)S(1)}, s32[768]{0:T(1024)}, u32[]{:S(2)}) copy-start(s32[768]{0:T(1024)} %row_ref.1) | copy-start | bytes 9220

commit v3 on v2

--- a/solution.py
+++ b/solution.py
@@ -28,13 +28,15 @@
     return -(-value // step) * step
 
 
-def owner_of(index, members, away):
-    if away is None:
+def owner_of(index, owners):
+    if owners is None:
         return index
-    return ((lax.axis_index("seq") + members + away[index // 2]) % members) ^ (index % 2)
-
-
-def prepare_kernel(members, away, row_ref, query_hbm, key_hbm, mask_ref, turned_ref, key_ref, query_ref, sem):
+    me = lax.axis_index("seq")
+    chip = sum(jnp.where(me // 2 == i, owner, 0) for i, owner in enumerate(owners[index // 2]))
+    return 2 * chip + ((me % 2) ^ (index % 2))
+
+
+def prepare_kernel(members, owners, row_ref, query_hbm, key_hbm, mask_ref, turned_ref, key_ref, query_ref, sem):
     rows, heads, depth = query_ref.shape
     groups, _, width = turned_ref.shape
     fetch_query = pltpu.make_async_copy(query_hbm, query_ref, sem.at[0])
@@ -52,13 +54,13 @@
     position = pltpu.roll(row_ref[...].reshape(1, total), back, 1)[:, :extra]
 
     def mask(index):
-        hidden = (place + owner_of(index, members, away) * block > position) & (column < rows)
+        hidden = (place + owner_of(index, owners) * block > position) & (column < rows)
         value = jnp.where(hidden, NEG, 0.0)
         here = index * block
-        here = here if away else pl.multiple_of(here, block)
+        here = here if owners else pl.multiple_of(here, block)
         mask_ref[pl.ds(here, block), :] = value.astype(mask_ref.dtype)
 
-    if away is None:
+    if owners is None:
         pl.loop(0, members)(mask)
     else:
         for index in range(members):
@@ -150,7 +152,7 @@
         tops[step] = jnp.max(top, axis=0, keepdims=True)
 
 
-def column_kernel(members, away, counts, copies, rows, early, mask_ref, turned_ref, *refs):
+def column_kernel(owners, counts, copies, rows, early, mask_ref, turned_ref, *refs):
     stages = [refs[3 * i : 3 * i + 3] for i in range(early)]
     refs = refs[3 * early :]
     key_refs, (out_ref, keys, plain, total, *scores) = refs[: len(counts)], refs[len(counts) :]
@@ -250,7 +252,7 @@
             lax.dot_general(ones, part, CONTRACT_LAST, preferred_element_type=jnp.float32)
             for part in (high, low)
         )[:1]
-        row = owner_of(index, members, away)
+        row = owner_of(index, owners)
         line = line * (1.0 / (width // rows))
         for i in range(copies):
             out_ref[i * (every // block) + row, :, :] = line
@@ -262,18 +264,28 @@
         pl.loop(0, every // block)(finish)
 
 
+def ring_of(chips):
+    return list(range(0, chips, 2)) + list(range(1, chips, 2))[::-1]
+
+
 def gather_keys(key_vectors):
     size = lax.axis_size("seq")
+    ring = ring_of(size // 2)
+    place = {chip: i for i, chip in enumerate(ring)}
+
+    def chip_at(chip, steps):
+        return ring[(place[chip] + steps) % len(ring)]
+
     swap = [(i, i ^ 1) for i in range(size)]
-    ahead = [(i, (i + 2) % size) for i in range(size)]
+    ahead = [(i, 2 * chip_at(i // 2, 1) + i % 2) for i in range(size)]
     blocks = {"own": key_vectors}
     blocks["left"] = lax.ppermute(key_vectors, "seq", ahead)
-    blocks["right"] = lax.ppermute(key_vectors, "seq", [(j, i) for i, j in ahead])
+    blocks["right"] = lax.ppermute(key_vectors, "seq", sorted((j, i) for i, j in ahead))
     blocks["far"] = lax.ppermute(blocks["left"], "seq", ahead)
     found = []
     for block in blocks.values():
         found += [block, lax.ppermute(block, "seq", swap)]
-    return found, (0, -2, 2, -4)
+    return found, [[chip_at(i, by) for i in range(size // 2)] for by in (0, -1, 1, -2)]
 
 
 def on_device(sampled_rows, query_vectors, key_vectors):
@@ -285,14 +297,14 @@
     amount = members * local_keys
     extra = round_up(local_rows, 128)
     if members == 8:
-        blocks, away = gather_keys(key_vectors)
+        blocks, owners = gather_keys(key_vectors)
         early, counts = 3, [1] * 2
     else:
-        blocks, away = [lax.all_gather(key_vectors, "seq", axis=0, tiled=True)], None
+        blocks, owners = [lax.all_gather(key_vectors, "seq", axis=0, tiled=True)], None
         early, counts = 0, [members]
     blocks = [b.reshape(-1, depth) for b in blocks]
     mask, turned, own = pl.pallas_call(
-        functools.partial(prepare_kernel, members, away),
+        functools.partial(prepare_kernel, members, owners),
         out_shape=(
             jax.ShapeDtypeStruct((amount, extra), jnp.bfloat16),
             jax.ShapeDtypeStruct((groups, depth + extra, width), jnp.bfloat16),
@@ -335,7 +347,7 @@
     blocks = blocks[2 * early :]
     left = sum(counts) * local_keys
     partial = pl.pallas_call(
-        functools.partial(column_kernel, members, away, counts, others, local_rows, early),
+        functools.partial(column_kernel, owners, counts, others, local_rows, early),
         out_shape=jax.ShapeDtypeStruct((others * members, 1, local_keys), jnp.float32),
         in_specs=[WHOLE] * (2 + len(stages) + len(blocks)),
         out_specs=WHOLE,

time: 35.7 us -> 35.1 us (0.983)
  waiting for transfers between devices: 10.8 us -> 6.23 us
  starting transfers between devices: 5.6 us -> 7.86 us
  blocking collectives: 11.1 us -> 12.7 us
    ppermute x1, waiting for transfers between devices: 5.37 us -> 2.02 us  [gather_keys(): blocks['far'] = lax.ppermute(blocks['left'], 'seq', ahead)]
    ppermute x1, starting transfers between devices: 0.01 us -> 3.28 us  [gather_keys(): blocks['far'] = lax.ppermute(blocks['left'], 'seq', ahead)]
    ppermute x1, starting transfers between devices: 2.03 us -> 0.01 us  [gather_keys(): lax.ppermute(key_vectors, 'seq', sorted(((j, i) for i, j in ahead)))]
    all_to_all x1, blocking collectives: 11.1 us -> 12.7 us  [on_device(): received = lax.all_to_all(partial, ('kv', 'seq'), 0, 0, tiled=True)]
    ppermute x1, starting transfers between devices: 3.05 us -> 4.06 us  [gather_keys(): blocks['left'] = lax.ppermute(key_vectors, 'seq', ahead)]
    ppermute x1, waiting for transfers between devices: 0.88 us -> 0.01 us  [gather_keys(): lax.ppermute(key_vectors, 'seq', sorted(((j, i) for i, j in ahead)))]
  transfers between devices with their start and end apart: 7 -> 7, of which waited for: 3 -> 2; matrix products, arithmetic and copies ran while one was open for 0% -> 0% of each run, Pallas kernels for 13% -> 13%
where the time goes in v3:
time: 35.1 us; the launch traced here: 34.9 us
  blocking collectives  12.7 us (36%)
  starting transfers between devices  7.86 us (22%)
  Pallas kernels  6.72 us (19%)
  waiting for transfers between devices  6.23 us (18%)
  local copies, waits for them, and re-layouts  0.69 us (2%)
  other arithmetic  0.62 us (2%)
    all_to_all x1, blocking collectives, on_device(): received = lax.all_to_all(partial, ('kv', 'seq'), 0, 0, tiled=True)  12.7 us
    ppermute x1, waiting for transfers between devices, gather_keys(): blocks['left'] = lax.ppermute(key_vectors, 'seq', ahead)  4.2 us
    ppermute x1, starting transfers between devices, gather_keys(): blocks['left'] = lax.ppermute(key_vectors, 'seq', ahead)  4.06 us
    ppermute x1, starting transfers between devices, gather_keys(): blocks['far'] = lax.ppermute(blocks['left'], 'seq', ahead)  3.28 us
    pallas_call x3, Pallas kernels, on_device(): pl.pallas_call(functools.partial(stage_kernel, i * some), out_shape=(jax....  3.24 us
    pallas_call x1, Pallas kernels, on_device(): pl.pallas_call(functools.partial(column_kernel, owners, counts, others, l...  2.17 us
    ppermute x1, waiting for transfers between devices, gather_keys(): blocks['far'] = lax.ppermute(blocks['left'], 'seq', ahead)  2.02 us
    pallas_call x1, Pallas kernels, on_device(): pl.pallas_call(functools.partial(prepare_kernel, members, owners), out_sh...  1.3 us
  transfers between devices with their start and end apart: 7, of which 2 were waited for; matrix products, arithmetic and copies ran while one was open for 0% of the time, Pallas kernels for 13%

profile of v3, /device:TPU:0, one launch (start us, length us, event | category | flops | bytes accessed | tf_op | source)
XLA Modules:
  0.0 34.9 jit_solution(1553302945998873050)
XLA Ops:
  0.0 4.1 %collective-permute-start.1 = (bf16[256,2,128]{2,1,0:T(2,128)(2,1)}, bf16[256,2,128]{2,1,0:T(2,128)(2,1)S(1)}, u32[]{:S(2)}, u32[]{:S(2)}) collective-permute-start(bf16[256,2,128]{2,1,0:T(2,128)(2,1)} %param.5), channel_id=1, source_target_pairs={{0,4},{1,5},{2,0},{3,1},{4,6},{5,7},{6,2},{7,3},{8,12},{9,13},{10,... | collective-permute-start | bytes 393224 | tf_op jit(solution)/shard_map/ppermute | solution.py:282
  4.1 0.0 collective-permute-start.3
  4.1 4.2 %collective-permute-done.1 = bf16[256,2,128]{2,1,0:T(2,128)(2,1)S(1)} collective-permute-done((bf16[256,2,128]{2,1,0:T(2,128)(2,1)}, bf16[256,2,128]{2,1,0:T(2,128)(2,1)S(1)}, u32[]{:S(2)}, u32[]{:S(2)}) %collective-permute-start.1) | collective-permute-done | bytes 131104 | tf_op jit(solution)/shard_map/ppermute | solution.py:282
  8.3 3.3 %collective-permute-start.5 = (bf16[256,2,128]{2,1,0:T(2,128)(2,1)S(1)}, bf16[256,2,128]{2,1,0:T(2,128)(2,1)S(1)}, u32[]{:S(2)}, u32[]{:S(2)}) collective-permute-start(bf16[256,2,128]{2,1,0:T(2,128)(2,1)S(1)} %collective-permute-done.1), channel_id=1, source_target_pairs={{0,4},{1,5},{2,0},{3,1},{4,6},{5,7},{6,2},{7,3},{8,12},{9,13},{10,... | collective-permute-start | bytes 393224 | tf_op jit(solution)/shard_map/ppermute | solution.py:284
  11.5 0.0 collective-permute-start
  11.6 0.5 %collective-permute-start.2 = (bf16[256,2,128]{2,1,0:T(2,128)(2,1)S(1)}, bf16[256,2,128]{2,1,0:T(2,128)(2,1)S(1)}, u32[]{:S(2)}, u32[]{:S(2)}) collective-permute-start(bf16[256,2,128]{2,1,0:T(2,128)(2,1)S(1)} %collective-permute-done.1), channel_id=1, source_target_pairs={{0,1},{1,0},{2,3},{3,2},{4,5},{5,4},{6,7},{7,6},{8,9},{9,8},{10,11... | collective-permute-start | bytes 393224 | tf_op jit(solution)/shard_map/ppermute | solution.py:287
  12.1 0.0 collective-permute-done.3
  12.1 0.0 collective-permute-start.4
  12.1 2.0 %collective-permute-done.5 = bf16[256,2,128]{2,1,0:T(2,128)(2,1)S(1)} collective-permute-done((bf16[256,2,128]{2,1,0:T(2,128)(2,1)S(1)}, bf16[256,2,128]{2,1,0:T(2,128)(2,1)S(1)}, u32[]{:S(2)}, u32[]{:S(2)}) %collective-permute-start.5) | collective-permute-done | bytes 131104 | tf_op jit(solution)/shard_map/ppermute | solution.py:284
  14.1 0.0 collective-permute-start.6
  14.1 0.0 copy-start
  14.1 0.7 %copy-done = s32[768]{0:T(1024)S(1)} copy-done((s32[768]{0:T(1024)S(1)}, s32[768]{0:T(1024)}, u32[]{:S(2)}) %copy-start) | copy-done | bytes 3096
  14.8 1.3 %prepare.1 = (bf16[2048,128]{1,0:T(8,128)(2,1)S(1)}, bf16[2,256,768]{2,1,0:T(8,128)(2,1)S(1)}, bf16[512,128]{1,0:T(8,128)(2,1)S(1)}) custom-call(s32[768]{0:T(1024)S(1)} %copy-done, bf16[96,16,128]{2,1,0:T(8,128)(2,1)} %query_hbm.1, bf16[512,128]{1,0:T(8,128)(2,1)} %bitcast.15), custom_call_target="tpu_custom_call" | custom-call | tf_op jit(solution)/shard_map/prepare/pallas_call | solution.py:306
  16.1 0.0 collective-permute-done
  16.1 1.1 %shard_map.37 = (f32[512,1536]{1,0:T(8,128)S(1)}, f32[1,1536]{1,0:T(1,128)S(1)}, f32[1,1536]{1,0:T(1,128)S(1)}) custom-call(bf16[2048,128]{1,0:T(8,128)(2,1)S(1)} %get-tuple-element.17.mask_ref, bf16[2,256,768]{2,1,0:T(8,128)(2,1)S(1)} %get-tuple-element.18.turned_ref, bf16[512,128]{1,0:T(8,128)(2,1)S(1)} %get-tuple-element.19.refs_0_, ...), custom_call_target="tpu_custom_call" | custom-call | tf_op jit(solution)/shard_map/pallas_call | solution.py:331
  17.2 0.0 collective-permute-done.2
  17.2 1.1 %shard_map.38 = (f32[512,1536]{1,0:T(8,128)S(1)}, f32[1,1536]{1,0:T(1,128)S(1)}, f32[1,1536]{1,0:T(1,128)S(1)}) custom-call(bf16[2048,128]{1,0:T(8,128)(2,1)S(1)} %get-tuple-element.17.mask_ref, bf16[2,256,768]{2,1,0:T(8,128)(2,1)S(1)} %get-tuple-element.18.turned_ref, bf16[512,128]{1,0:T(8,128)(2,1)S(1)} %bitcast.11, bf16[512,128]{1,0:T(8,128)(2,1)S(1)} %bitcast.13), custom_call_target="tpu_custom_call" | custom-call | tf_op jit(solution)/shard_map/pallas_call | solution.py:331
  18.3 0.0 collective-permute-done.4
  18.3 1.1 %shard_map.39 = (f32[512,1536]{1,0:T(8,128)S(1)}, f32[1,1536]{1,0:T(1,128)S(1)}, f32[1,1536]{1,0:T(1,128)S(1)}) custom-call(bf16[2048,128]{1,0:T(8,128)(2,1)S(1)} %get-tuple-element.17.mask_ref, bf16[2,256,768]{2,1,0:T(8,128)(2,1)S(1)} %get-tuple-element.18.turned_ref, bf16[512,128]{1,0:T(8,128)(2,1)S(1)} %bitcast.10, bf16[512,128]{1,0:T(8,128)(2,1)S(1)} %bitcast.12), custom_call_target="tpu_custom_call" | custom-call | tf_op jit(solution)/shard_map/pallas_call | solution.py:331
  19.4 0.0 collective-permute-done.6
  19.4 2.2 %columns.1 = f32[32,1,256]{2,1,0:T(1,128)S(1)} custom-call(bf16[2048,128]{1,0:T(8,128)(2,1)S(1)} %get-tuple-element.17.mask_ref, bf16[2,256,768]{2,1,0:T(8,128)(2,1)S(1)} %get-tuple-element.18.turned_ref, f32[512,1536]{1,0:T(8,128)S(1)} %get-tuple-element.20.refs_0_, f32[1,1536]{1,0:T(1,128)S(1)} %get-tuple-element.21.refs_1_, ...), custom_call_target="tpu_custom_call" | custom-call | tf_op jit(solution)/shard_map/columns/pallas_call | solution.py:349
  21.5 12.7 %all_to_all.5 = f32[32,1,256]{2,1,0:T(1,128)S(1)} all-to-all(f32[32,1,256]{2,1,0:T(1,128)S(1)} %columns.1), channel_id=1, replica_groups=mesh['kv'=4,'seq'=8] {'kv','seq'}, dimensions={0} | all-to-all | bytes 65536 | tf_op jit(solution)/shard_map/all_to_all | solution.py:363
  34.3 0.6 %reduce_sum.9 = f32[256]{0:T(256)} reduce(f32[32,1,256]{2,1,0:T(1,128)S(1)} %all_to_all.5, f32[]{:T(128)} %constant.0.clone.1), dimensions={0,1}, to_apply=%region_0.0 | reduce | flops 7936 | bytes 33796 | tf_op jit(solution)/shard_map/reduce_sum | solution.py:364
Async XLA Ops:
  0.0 8.3 %collective-permute-start.1 = (bf16[256,2,128]{2,1,0:T(2,128)(2,1)}, bf16[256,2,128]{2,1,0:T(2,128)(2,1)S(1)}, u32[]{:S(2)}, u32[]{:S(2)}) collective-permute-start(bf16[256,2,128]{2,1,0:T(2,128)(2,1)} %param.5), channel_id=1, source_target_pairs={{0,4},{1,5},{2,0},{3,1},{4,6},{5,7},{6,2},{7,3},{8,12},{9,13},{10,... | collective-permute-start | bytes 393224 | tf_op jit(solution)/shard_map/ppermute | solution.py:282
  4.1 8.0 %collective-permute-start.3 = (bf16[256,2,128]{2,1,0:T(2,128)(2,1)}, bf16[256,2,128]{2,1,0:T(2,128)(2,1)S(1)}, u32[]{:S(2)}, u32[]{:S(2)}) collective-permute-start(bf16[256,2,128]{2,1,0:T(2,128)(2,1)} %param.5), channel_id=1, source_target_pairs={{0,2},{1,3},{2,6},{3,7},{4,0},{5,1},{6,4},{7,5},{8,10},{9,11},{10,... | collective-permute-start | bytes 393224 | tf_op jit(solution)/shard_map/ppermute | solution.py:283
  8.3 5.8 %collective-permute-start.5 = (bf16[256,2,128]{2,1,0:T(2,128)(2,1)S(1)}, bf16[256,2,128]{2,1,0:T(2,128)(2,1)S(1)}, u32[]{:S(2)}, u32[]{:S(2)}) collective-permute-start(bf16[256,2,128]{2,1,0:T(2,128)(2,1)S(1)} %collective-permute-done.1), channel_id=1, source_target_pairs={{0,4},{1,5},{2,0},{3,1},{4,6},{5,7},{6,2},{7,3},{8,12},{9,13},{10,... | collective-permute-start | bytes 393224 | tf_op jit(solution)/shard_map/ppermute | solution.py:284
  11.5 4.5 %collective-permute-start = (bf16[256,2,128]{2,1,0:T(2,128)(2,1)}, bf16[256,2,128]{2,1,0:T(2,128)(2,1)S(1)}, u32[]{:S(2)}, u32[]{:S(2)}) collective-permute-start(bf16[256,2,128]{2,1,0:T(2,128)(2,1)} %param.5), channel_id=1, source_target_pairs={{0,1},{1,0},{2,3},{3,2},{4,5},{5,4},{6,7},{7,6},{8,9},{9,8},{10,11... | collective-permute-start | bytes 393224 | tf_op jit(solution)/shard_map/ppermute | solution.py:287
  11.6 5.6 %collective-permute-start.2 = (bf16[256,2,128]{2,1,0:T(2,128)(2,1)S(1)}, bf16[256,2,128]{2,1,0:T(2,128)(2,1)S(1)}, u32[]{:S(2)}, u32[]{:S(2)}) collective-permute-start(bf16[256,2,128]{2,1,0:T(2,128)(2,1)S(1)} %collective-permute-done.1), channel_id=1, source_target_pairs={{0,1},{1,0},{2,3},{3,2},{4,5},{5,4},{6,7},{7,6},{8,9},{9,8},{10,11... | collective-permute-start | bytes 393224 | tf_op jit(solution)/shard_map/ppermute | solution.py:287
  12.1 6.2 %collective-permute-start.4 = (bf16[256,2,128]{2,1,0:T(2,128)(2,1)S(1)}, bf16[256,2,128]{2,1,0:T(2,128)(2,1)S(1)}, u32[]{:S(2)}, u32[]{:S(2)}) collective-permute-start(bf16[256,2,128]{2,1,0:T(2,128)(2,1)S(1)} %collective-permute-done.3), channel_id=1, source_target_pairs={{0,1},{1,0},{2,3},{3,2},{4,5},{5,4},{6,7},{7,6},{8,9},{9,8},{10,11... | collective-permute-start | bytes 393224 | tf_op jit(solution)/shard_map/ppermute | solution.py:287
  14.1 5.3 %collective-permute-start.6 = (bf16[256,2,128]{2,1,0:T(2,128)(2,1)S(1)}, bf16[256,2,128]{2,1,0:T(2,128)(2,1)S(1)}, u32[]{:S(2)}, u32[]{:S(2)}) collective-permute-start(bf16[256,2,128]{2,1,0:T(2,128)(2,1)S(1)} %collective-permute-done.5), channel_id=1, source_target_pairs={{0,1},{1,0},{2,3},{3,2},{4,5},{5,4},{6,7},{7,6},{8,9},{9,8},{10,11... | collective-permute-start | bytes 393224 | tf_op jit(solution)/shard_map/ppermute | solution.py:287
  14.1 0.7 %copy-start = (s32[768]{0:T(1024)S(1)}, s32[768]{0:T(1024)}, u32[]{:S(2)}) copy-start(s32[768]{0:T(1024)} %row_ref.1) | copy-start | bytes 9220

commit v4 on v3

--- a/solution.py
+++ b/solution.py
@@ -13,7 +13,7 @@
 LOW = -1e20
 SPAN = 2048
 LANES = 256
-CHUNK = 256
+CHUNK = 128
 CONTRACT_LAST = (((1,), (1,)), ((), ()))
 CONTRACT_INNER = (((1,), (0,)), ((), ()))
 WHOLE = pl.BlockSpec(memory_space=pltpu.VMEM)
@@ -298,10 +298,10 @@
     extra = round_up(local_rows, 128)
     if members == 8:
         blocks, owners = gather_keys(key_vectors)
-        early, counts = 3, [1] * 2
+        early, counts = [2, 2, 2, 1], [1]
     else:
         blocks, owners = [lax.all_gather(key_vectors, "seq", axis=0, tiled=True)], None
-        early, counts = 0, [members]
+        early, counts = [], [members]
     blocks = [b.reshape(-1, depth) for b in blocks]
     mask, turned, own = pl.pallas_call(
         functools.partial(prepare_kernel, members, owners),
@@ -326,16 +326,16 @@
     if early:
         blocks[0] = own
     stages = []
-    some = 2 * local_keys
-    for i in range(early):
+    for i, blocks_here in enumerate(early):
+        first, some = sum(early[:i]), blocks_here * local_keys
         stages += pl.pallas_call(
-            functools.partial(stage_kernel, i * some),
+            functools.partial(stage_kernel, first * local_keys),
             out_shape=(
                 jax.ShapeDtypeStruct((some, groups * width), jnp.float32),
                 jax.ShapeDtypeStruct((1, groups * width), jnp.float32),
                 jax.ShapeDtypeStruct((1, groups * width), jnp.float32),
             ),
-            in_specs=[WHOLE] * 4,
+            in_specs=[WHOLE] * (2 + blocks_here),
             out_specs=(WHOLE,) * 3,
             scratch_shapes=[
                 pltpu.VMEM((groups, some, depth), jnp.bfloat16),
@@ -343,11 +343,11 @@
             ]
             + [pltpu.VMEM((some, LANES), jnp.float32)] * 2,
             compiler_params=grant(12),
-        )(mask, turned, *blocks[2 * i : 2 * i + 2])
-    blocks = blocks[2 * early :]
+        )(mask, turned, *blocks[first : first + blocks_here])
+    blocks = blocks[sum(early) :]
     left = sum(counts) * local_keys
     partial = pl.pallas_call(
-        functools.partial(column_kernel, owners, counts, others, local_rows, early),
+        functools.partial(column_kernel, owners, counts, others, local_rows, len(early)),
         out_shape=jax.ShapeDtypeStruct((others * members, 1, local_keys), jnp.float32),
         in_specs=[WHOLE] * (2 + len(stages) + len(blocks)),
         out_specs=WHOLE,

time: 35.1 us -> 35.2 us (level)
    pallas_call x3 -> x4, Pallas kernels: 3.24 us -> 3.87 us  [on_device(): pl.pallas_call(functools.partial(stage_kernel, first * local_keys), out_s...]
    pallas_call x1, Pallas kernels: 2.17 us -> 1.65 us  [on_device(): pl.pallas_call(functools.partial(column_kernel, owners, counts, others, l...]
  transfers between devices with their start and end apart: 7 -> 7, of which waited for: 2 -> 2; matrix products, arithmetic and copies ran while one was open for 0% -> 0% of each run, Pallas kernels for 13% -> 15%
where the time goes in v4:
time: 35.2 us; the launch traced here: 35 us
  blocking collectives  12.7 us (36%)
  starting transfers between devices  7.86 us (22%)
  Pallas kernels  6.83 us (19%)
  waiting for transfers between devices  6.23 us (18%)
  local copies, waits for them, and re-layouts  0.69 us (2%)
  other arithmetic  0.62 us (2%)
    all_to_all x1, blocking collectives, on_device(): received = lax.all_to_all(partial, ('kv', 'seq'), 0, 0, tiled=True)  12.7 us
    ppermute x1, waiting for transfers between devices, gather_keys(): blocks['left'] = lax.ppermute(key_vectors, 'seq', ahead)  4.2 us
    ppermute x1, starting transfers between devices, gather_keys(): blocks['left'] = lax.ppermute(key_vectors, 'seq', ahead)  4.06 us
    pallas_call x4, Pallas kernels, on_device(): pl.pallas_call(functools.partial(stage_kernel, first * local_keys), out_s...  3.87 us
    ppermute x1, starting transfers between devices, gather_keys(): blocks['far'] = lax.ppermute(blocks['left'], 'seq', ahead)  3.28 us
    ppermute x1, waiting for transfers between devices, gather_keys(): blocks['far'] = lax.ppermute(blocks['left'], 'seq', ahead)  2.02 us
    pallas_call x1, Pallas kernels, on_device(): pl.pallas_call(functools.partial(column_kernel, owners, counts, others, l...  1.65 us
    pallas_call x1, Pallas kernels, on_device(): pl.pallas_call(functools.partial(prepare_kernel, members, owners), out_sh...  1.3 us
  transfers between devices with their start and end apart: 7, of which 2 were waited for; matrix products, arithmetic and copies ran while one was open for 0% of the time, Pallas kernels for 15%

profile of v4, /device:TPU:0, one launch (start us, length us, event | category | flops | bytes accessed | tf_op | source)
XLA Modules:
  0.0 35.0 jit_solution(16824226965070008227)
XLA Ops:
  0.0 4.1 %collective-permute-start.1 = (bf16[256,2,128]{2,1,0:T(2,128)(2,1)}, bf16[256,2,128]{2,1,0:T(2,128)(2,1)S(1)}, u32[]{:S(2)}, u32[]{:S(2)}) collective-permute-start(bf16[256,2,128]{2,1,0:T(2,128)(2,1)} %param.5), channel_id=1, source_target_pairs={{0,4},{1,5},{2,0},{3,1},{4,6},{5,7},{6,2},{7,3},{8,12},{9,13},{10,... | collective-permute-start | bytes 393224 | tf_op jit(solution)/shard_map/ppermute | solution.py:282
  4.1 0.0 collective-permute-start.3
  4.1 4.2 %collective-permute-done.1 = bf16[256,2,128]{2,1,0:T(2,128)(2,1)S(1)} collective-permute-done((bf16[256,2,128]{2,1,0:T(2,128)(2,1)}, bf16[256,2,128]{2,1,0:T(2,128)(2,1)S(1)}, u32[]{:S(2)}, u32[]{:S(2)}) %collective-permute-start.1) | collective-permute-done | bytes 131104 | tf_op jit(solution)/shard_map/ppermute | solution.py:282
  8.3 3.3 %collective-permute-start.5 = (bf16[256,2,128]{2,1,0:T(2,128)(2,1)S(1)}, bf16[256,2,128]{2,1,0:T(2,128)(2,1)S(1)}, u32[]{:S(2)}, u32[]{:S(2)}) collective-permute-start(bf16[256,2,128]{2,1,0:T(2,128)(2,1)S(1)} %collective-permute-done.1), channel_id=1, source_target_pairs={{0,4},{1,5},{2,0},{3,1},{4,6},{5,7},{6,2},{7,3},{8,12},{9,13},{10,... | collective-permute-start | bytes 393224 | tf_op jit(solution)/shard_map/ppermute | solution.py:284
  11.5 0.0 collective-permute-start
  11.6 0.5 %collective-permute-start.2 = (bf16[256,2,128]{2,1,0:T(2,128)(2,1)S(1)}, bf16[256,2,128]{2,1,0:T(2,128)(2,1)S(1)}, u32[]{:S(2)}, u32[]{:S(2)}) collective-permute-start(bf16[256,2,128]{2,1,0:T(2,128)(2,1)S(1)} %collective-permute-done.1), channel_id=1, source_target_pairs={{0,1},{1,0},{2,3},{3,2},{4,5},{5,4},{6,7},{7,6},{8,9},{9,8},{10,11... | collective-permute-start | bytes 393224 | tf_op jit(solution)/shard_map/ppermute | solution.py:287
  12.1 0.0 collective-permute-done.3
  12.1 0.0 collective-permute-start.4
  12.1 2.0 %collective-permute-done.5 = bf16[256,2,128]{2,1,0:T(2,128)(2,1)S(1)} collective-permute-done((bf16[256,2,128]{2,1,0:T(2,128)(2,1)S(1)}, bf16[256,2,128]{2,1,0:T(2,128)(2,1)S(1)}, u32[]{:S(2)}, u32[]{:S(2)}) %collective-permute-start.5) | collective-permute-done | bytes 131104 | tf_op jit(solution)/shard_map/ppermute | solution.py:284
  14.1 0.0 collective-permute-start.6
  14.1 0.0 copy-start
  14.1 0.7 %copy-done = s32[768]{0:T(1024)S(1)} copy-done((s32[768]{0:T(1024)S(1)}, s32[768]{0:T(1024)}, u32[]{:S(2)}) %copy-start) | copy-done | bytes 3096
  14.8 1.3 %prepare.1 = (bf16[2048,128]{1,0:T(8,128)(2,1)S(1)}, bf16[2,256,768]{2,1,0:T(8,128)(2,1)S(1)}, bf16[512,128]{1,0:T(8,128)(2,1)S(1)}) custom-call(s32[768]{0:T(1024)S(1)} %copy-done, bf16[96,16,128]{2,1,0:T(8,128)(2,1)} %query_hbm.1, bf16[512,128]{1,0:T(8,128)(2,1)} %bitcast.15), custom_call_target="tpu_custom_call" | custom-call | tf_op jit(solution)/shard_map/prepare/pallas_call | solution.py:306
  16.1 0.0 collective-permute-done
  16.1 1.1 %shard_map.37 = (f32[512,1536]{1,0:T(8,128)S(1)}, f32[1,1536]{1,0:T(1,128)S(1)}, f32[1,1536]{1,0:T(1,128)S(1)}) custom-call(bf16[2048,128]{1,0:T(8,128)(2,1)S(1)} %get-tuple-element.20.mask_ref, bf16[2,256,768]{2,1,0:T(8,128)(2,1)S(1)} %get-tuple-element.21.turned_ref, bf16[512,128]{1,0:T(8,128)(2,1)S(1)} %get-tuple-element.22.refs_0_, ...), custom_call_target="tpu_custom_call" | custom-call | tf_op jit(solution)/shard_map/pallas_call | solution.py:331
  17.2 0.6 %shard_map.40 = (f32[256,1536]{1,0:T(8,128)S(1)}, f32[1,1536]{1,0:T(1,128)S(1)}, f32[1,1536]{1,0:T(1,128)S(1)}) custom-call(bf16[2048,128]{1,0:T(8,128)(2,1)S(1)} %get-tuple-element.20.mask_ref, bf16[2,256,768]{2,1,0:T(8,128)(2,1)S(1)} %get-tuple-element.21.turned_ref, bf16[512,128]{1,0:T(8,128)(2,1)S(1)} %bitcast.14), custom_call_target="tpu_custom_call" | custom-call | tf_op jit(solution)/shard_map/pallas_call | solution.py:331
  17.8 0.0 collective-permute-done.2
  17.8 1.1 %shard_map.38 = (f32[512,1536]{1,0:T(8,128)S(1)}, f32[1,1536]{1,0:T(1,128)S(1)}, f32[1,1536]{1,0:T(1,128)S(1)}) custom-call(bf16[2048,128]{1,0:T(8,128)(2,1)S(1)} %get-tuple-element.20.mask_ref, bf16[2,256,768]{2,1,0:T(8,128)(2,1)S(1)} %get-tuple-element.21.turned_ref, bf16[512,128]{1,0:T(8,128)(2,1)S(1)} %bitcast.10, bf16[512,128]{1,0:T(8,128)(2,1)S(1)} %bitcast.12), custom_call_target="tpu_custom_call" | custom-call | tf_op jit(solution)/shard_map/pallas_call | solution.py:331
  18.9 0.0 collective-permute-done.4
  18.9 1.1 %shard_map.39 = (f32[512,1536]{1,0:T(8,128)S(1)}, f32[1,1536]{1,0:T(1,128)S(1)}, f32[1,1536]{1,0:T(1,128)S(1)}) custom-call(bf16[2048,128]{1,0:T(8,128)(2,1)S(1)} %get-tuple-element.20.mask_ref, bf16[2,256,768]{2,1,0:T(8,128)(2,1)S(1)} %get-tuple-element.21.turned_ref, bf16[512,128]{1,0:T(8,128)(2,1)S(1)} %bitcast.9, bf16[512,128]{1,0:T(8,128)(2,1)S(1)} %bitcast.11), custom_call_target="tpu_custom_call" | custom-call | tf_op jit(solution)/shard_map/pallas_call | solution.py:331
  20.0 0.0 collective-permute-done.6
  20.0 1.7 %columns.1 = f32[32,1,256]{2,1,0:T(1,128)S(1)} custom-call(bf16[2048,128]{1,0:T(8,128)(2,1)S(1)} %get-tuple-element.20.mask_ref, bf16[2,256,768]{2,1,0:T(8,128)(2,1)S(1)} %get-tuple-element.21.turned_ref, f32[512,1536]{1,0:T(8,128)S(1)} %get-tuple-element.23.refs_0_, f32[1,1536]{1,0:T(1,128)S(1)} %get-tuple-element.24.refs_1_, ...), custom_call_target="tpu_custom_call" | custom-call | tf_op jit(solution)/shard_map/columns/pallas_call | solution.py:349
  21.6 12.7 %all_to_all.5 = f32[32,1,256]{2,1,0:T(1,128)S(1)} all-to-all(f32[32,1,256]{2,1,0:T(1,128)S(1)} %columns.1), channel_id=1, replica_groups=mesh['kv'=4,'seq'=8] {'kv','seq'}, dimensions={0} | all-to-all | bytes 65536 | tf_op jit(solution)/shard_map/all_to_all | solution.py:363
  34.4 0.6 %reduce_sum.9 = f32[256]{0:T(256)} reduce(f32[32,1,256]{2,1,0:T(1,128)S(1)} %all_to_all.5, f32[]{:T(128)} %constant.0.clone.1), dimensions={0,1}, to_apply=%region_0.0 | reduce | flops 7936 | bytes 33796 | tf_op jit(solution)/shard_map/reduce_sum | solution.py:364
Async XLA Ops:
  0.0 8.3 %collective-permute-start.1 = (bf16[256,2,128]{2,1,0:T(2,128)(2,1)}, bf16[256,2,128]{2,1,0:T(2,128)(2,1)S(1)}, u32[]{:S(2)}, u32[]{:S(2)}) collective-permute-start(bf16[256,2,128]{2,1,0:T(2,128)(2,1)} %param.5), channel_id=1, source_target_pairs={{0,4},{1,5},{2,0},{3,1},{4,6},{5,7},{6,2},{7,3},{8,12},{9,13},{10,... | collective-permute-start | bytes 393224 | tf_op jit(solution)/shard_map/ppermute | solution.py:282
  4.1 8.0 %collective-permute-start.3 = (bf16[256,2,128]{2,1,0:T(2,128)(2,1)}, bf16[256,2,128]{2,1,0:T(2,128)(2,1)S(1)}, u32[]{:S(2)}, u32[]{:S(2)}) collective-permute-start(bf16[256,2,128]{2,1,0:T(2,128)(2,1)} %param.5), channel_id=1, source_target_pairs={{0,2},{1,3},{2,6},{3,7},{4,0},{5,1},{6,4},{7,5},{8,10},{9,11},{10,... | collective-permute-start | bytes 393224 | tf_op jit(solution)/shard_map/ppermute | solution.py:283
  8.3 5.8 %collective-permute-start.5 = (bf16[256,2,128]{2,1,0:T(2,128)(2,1)S(1)}, bf16[256,2,128]{2,1,0:T(2,128)(2,1)S(1)}, u32[]{:S(2)}, u32[]{:S(2)}) collective-permute-start(bf16[256,2,128]{2,1,0:T(2,128)(2,1)S(1)} %collective-permute-done.1), channel_id=1, source_target_pairs={{0,4},{1,5},{2,0},{3,1},{4,6},{5,7},{6,2},{7,3},{8,12},{9,13},{10,... | collective-permute-start | bytes 393224 | tf_op jit(solution)/shard_map/ppermute | solution.py:284
  11.5 4.5 %collective-permute-start = (bf16[256,2,128]{2,1,0:T(2,128)(2,1)}, bf16[256,2,128]{2,1,0:T(2,128)(2,1)S(1)}, u32[]{:S(2)}, u32[]{:S(2)}) collective-permute-start(bf16[256,2,128]{2,1,0:T(2,128)(2,1)} %param.5), channel_id=1, source_target_pairs={{0,1},{1,0},{2,3},{3,2},{4,5},{5,4},{6,7},{7,6},{8,9},{9,8},{10,11... | collective-permute-start | bytes 393224 | tf_op jit(solution)/shard_map/ppermute | solution.py:287
  11.6 6.2 %collective-permute-start.2 = (bf16[256,2,128]{2,1,0:T(2,128)(2,1)S(1)}, bf16[256,2,128]{2,1,0:T(2,128)(2,1)S(1)}, u32[]{:S(2)}, u32[]{:S(2)}) collective-permute-start(bf16[256,2,128]{2,1,0:T(2,128)(2,1)S(1)} %collective-permute-done.1), channel_id=1, source_target_pairs={{0,1},{1,0},{2,3},{3,2},{4,5},{5,4},{6,7},{7,6},{8,9},{9,8},{10,11... | collective-permute-start | bytes 393224 | tf_op jit(solution)/shard_map/ppermute | solution.py:287
  12.1 6.8 %collective-permute-start.4 = (bf16[256,2,128]{2,1,0:T(2,128)(2,1)S(1)}, bf16[256,2,128]{2,1,0:T(2,128)(2,1)S(1)}, u32[]{:S(2)}, u32[]{:S(2)}) collective-permute-start(bf16[256,2,128]{2,1,0:T(2,128)(2,1)S(1)} %collective-permute-done.3), channel_id=1, source_target_pairs={{0,1},{1,0},{2,3},{3,2},{4,5},{5,4},{6,7},{7,6},{8,9},{9,8},{10,11... | collective-permute-start | bytes 393224 | tf_op jit(solution)/shard_map/ppermute | solution.py:287
  14.1 5.9 %collective-permute-start.6 = (bf16[256,2,128]{2,1,0:T(2,128)(2,1)S(1)}, bf16[256,2,128]{2,1,0:T(2,128)(2,1)S(1)}, u32[]{:S(2)}, u32[]{:S(2)}) collective-permute-start(bf16[256,2,128]{2,1,0:T(2,128)(2,1)S(1)} %collective-permute-done.5), channel_id=1, source_target_pairs={{0,1},{1,0},{2,3},{3,2},{4,5},{5,4},{6,7},{7,6},{8,9},{9,8},{10,11... | collective-permute-start | bytes 393224 | tf_op jit(solution)/shard_map/ppermute | solution.py:287
  14.1 0.7 %copy-start = (s32[768]{0:T(1024)S(1)}, s32[768]{0:T(1024)}, u32[]{:S(2)}) copy-start(s32[768]{0:T(1024)} %row_ref.1) | copy-start | bytes 9220

commit v5 on v4

--- a/solution.py
+++ b/solution.py
@@ -268,6 +268,19 @@
     return list(range(0, chips, 2)) + list(range(1, chips, 2))[::-1]
 
 
+def pick_kernel(ends, near_ref, far_ref, out_ref):
+    chip = lax.axis_index("seq") // 2
+    outer = (chip == ends[0]) | (chip == ends[1])
+
+    @pl.when(outer)
+    def _():
+        out_ref[...] = far_ref[...]
+
+    @pl.when(jnp.logical_not(outer))
+    def _():
+        out_ref[...] = near_ref[...]
+
+
 def gather_keys(key_vectors):
     size = lax.axis_size("seq")
     ring = ring_of(size // 2)
@@ -281,7 +294,19 @@
     blocks = {"own": key_vectors}
     blocks["left"] = lax.ppermute(key_vectors, "seq", ahead)
     blocks["right"] = lax.ppermute(key_vectors, "seq", sorted((j, i) for i, j in ahead))
-    blocks["far"] = lax.ppermute(blocks["left"], "seq", ahead)
+    ends = (0, size // 2 - 1)
+    beside = [(i, i ^ 1 if i // 2 in ends else i ^ 6) for i in range(size)]
+    near = lax.ppermute(key_vectors, "seq", beside)
+    far = lax.ppermute(blocks["left"], "seq", [(i, i ^ 2) for i in range(size)])
+    flat = [b.reshape(-1, b.shape[-1]) for b in (near, far)]
+    blocks["far"] = pl.pallas_call(
+        functools.partial(pick_kernel, ends),
+        out_shape=jax.ShapeDtypeStruct(flat[0].shape, near.dtype),
+        in_specs=[WHOLE] * 2,
+        out_specs=WHOLE,
+        compiler_params=grant(2),
+        name="pick",
+    )(*flat).reshape(near.shape)
     found = []
     for block in blocks.values():
         found += [block, lax.ppermute(block, "seq", swap)]
@@ -342,7 +367,7 @@
                 pltpu.VMEM((groups * local_keys, depth), jnp.float32),
             ]
             + [pltpu.VMEM((some, LANES), jnp.float32)] * 2,
-            compiler_params=grant(12),
+            compiler_params=grant(8),
         )(mask, turned, *blocks[first : first + blocks_here])
     blocks = blocks[sum(early) :]
     left = sum(counts) * local_keys
@@ -357,7 +382,7 @@
             pltpu.VMEM((amount, 128), jnp.float32),
         ]
         + [pltpu.VMEM((left, LANES), jnp.float32)] * (3 if left <= SPAN else 1),
-        compiler_params=grant(24 if left <= SPAN else 60),
+        compiler_params=grant(10 if left <= SPAN else 60),
         name="columns",
     )(mask, turned, *stages, *blocks)
     received = lax.all_to_all(partial, ("kv", "seq"), 0, 0, tiled=True)

time: 35.2 us -> 34.7 us (0.986)
  waiting for transfers between devices: 6.23 us -> 7.25 us
  starting transfers between devices: 7.86 us -> 6.91 us
  blocking collectives: 12.7 us -> 12.1 us
    ppermute x1, waiting for transfers between devices: 0.01 us -> 1.17 us  [gather_keys(): lax.ppermute(key_vectors, 'seq', sorted(((j, i) for i, j in ahead)))]
    ppermute x1 -> x2, starting transfers between devices: 3.28 us -> 2.26 us  [the longest x1 2.26 us: gather_keys(): far = lax.ppermute(blocks['left'], 'seq', [(i, i ^ 2) for i in range(size)])]
    all_to_all x1, blocking collectives: 12.7 us -> 12.1 us  [on_device(): received = lax.all_to_all(partial, ('kv', 'seq'), 0, 0, tiled=True)]
    ppermute x1 -> x2, waiting for transfers between devices: 2.02 us -> 1.87 us  [the longest x1 1.87 us: gather_keys(): far = lax.ppermute(blocks['left'], 'seq', [(i, i ^ 2) for i in range(size)])]
  transfers between devices with their start and end apart: 7 -> 8, of which waited for: 2 -> 3; matrix products, arithmetic and copies ran while one was open for 0% -> 0% of each run, Pallas kernels for 15% -> 15%
where the time goes in v5:
time: 34.7 us; the launch traced here: 34.5 us
  blocking collectives  12.1 us (35%)
  waiting for transfers between devices  7.25 us (21%)
  starting transfers between devices  6.91 us (20%)
  Pallas kernels  6.86 us (20%)
  local copies, waits for them, and re-layouts  0.68 us (2%)
  other arithmetic  0.62 us (2%)
    all_to_all x1, blocking collectives, on_device(): received = lax.all_to_all(partial, ('kv', 'seq'), 0, 0, tiled=True)  12.1 us
    ppermute x1, waiting for transfers between devices, gather_keys(): blocks['left'] = lax.ppermute(key_vectors, 'seq', ahead)  4.2 us
    ppermute x1, starting transfers between devices, gather_keys(): blocks['left'] = lax.ppermute(key_vectors, 'seq', ahead)  4.06 us
    pallas_call x4, Pallas kernels, on_device(): pl.pallas_call(functools.partial(stage_kernel, first * local_keys), out_s...  3.9 us
    ppermute x1, starting transfers between devices, gather_keys(): far = lax.ppermute(blocks['left'], 'seq', [(i, i ^ 2) for i in range(size)])  2.26 us
    ppermute x1, waiting for transfers between devices, gather_keys(): far = lax.ppermute(blocks['left'], 'seq', [(i, i ^ 2) for i in range(size)])  1.87 us
    pallas_call x1, Pallas kernels, on_device(): pl.pallas_call(functools.partial(column_kernel, owners, counts, others, l...  1.65 us
    pallas_call x1, Pallas kernels, on_device(): pl.pallas_call(functools.partial(prepare_kernel, members, owners), out_sh...  1.3 us
  transfers between devices with their start and end apart: 8, of which 3 were waited for; matrix products, arithmetic and copies ran while one was open for 0% of the time, Pallas kernels for 15%

profile of v5, /device:TPU:0, one launch (start us, length us, event | category | flops | bytes accessed | tf_op | source)
XLA Modules:
  0.0 34.5 jit_solution(5632273782268685998)
XLA Ops:
  0.0 4.1 %collective-permute-start.1 = (bf16[256,2,128]{2,1,0:T(2,128)(2,1)}, bf16[256,2,128]{2,1,0:T(2,128)(2,1)S(1)}, u32[]{:S(2)}, u32[]{:S(2)}) collective-permute-start(bf16[256,2,128]{2,1,0:T(2,128)(2,1)} %param.5), channel_id=1, source_target_pairs={{0,4},{1,5},{2,0},{3,1},{4,6},{5,7},{6,2},{7,3},{8,12},{9,13},{10,... | collective-permute-start | bytes 393224 | tf_op jit(solution)/shard_map/ppermute | solution.py:295
  4.1 0.0 collective-permute-start.3
  4.1 0.0 collective-permute-start.5
  4.1 4.2 %collective-permute-done.1 = bf16[256,2,128]{2,1,0:T(2,128)(2,1)S(1)} collective-permute-done((bf16[256,2,128]{2,1,0:T(2,128)(2,1)}, bf16[256,2,128]{2,1,0:T(2,128)(2,1)S(1)}, u32[]{:S(2)}, u32[]{:S(2)}) %collective-permute-start.1) | collective-permute-done | bytes 131104 | tf_op jit(solution)/shard_map/ppermute | solution.py:295
  8.3 2.3 %collective-permute-start.6 = (bf16[256,2,128]{2,1,0:T(2,128)(2,1)S(1)}, bf16[256,2,128]{2,1,0:T(2,128)(2,1)S(1)}, u32[]{:S(2)}, u32[]{:S(2)}) collective-permute-start(bf16[256,2,128]{2,1,0:T(2,128)(2,1)S(1)} %collective-permute-done.1), channel_id=1, source_target_pairs={{0,2},{1,3},{2,0},{3,1},{4,6},{5,7},{6,4},{7,5},{8,10},{9,11},{10,... | collective-permute-start | bytes 393224 | tf_op jit(solution)/shard_map/ppermute | solution.py:300
  10.5 0.0 collective-permute-start
  10.5 0.5 %collective-permute-start.2 = (bf16[256,2,128]{2,1,0:T(2,128)(2,1)S(1)}, bf16[256,2,128]{2,1,0:T(2,128)(2,1)S(1)}, u32[]{:S(2)}, u32[]{:S(2)}) collective-permute-start(bf16[256,2,128]{2,1,0:T(2,128)(2,1)S(1)} %collective-permute-done.1), channel_id=1, source_target_pairs={{0,1},{1,0},{2,3},{3,2},{4,5},{5,4},{6,7},{7,6},{8,9},{9,8},{10,11... | collective-permute-start | bytes 393224 | tf_op jit(solution)/shard_map/ppermute | solution.py:312
  11.0 1.2 %collective-permute-done.3 = bf16[256,2,128]{2,1,0:T(2,128)(2,1)S(1)} collective-permute-done((bf16[256,2,128]{2,1,0:T(2,128)(2,1)}, bf16[256,2,128]{2,1,0:T(2,128)(2,1)S(1)}, u32[]{:S(2)}, u32[]{:S(2)}) %collective-permute-start.3) | collective-permute-done | bytes 131104 | tf_op jit(solution)/shard_map/ppermute | solution.py:296
  12.2 0.0 collective-permute-start.4
  12.2 1.9 %collective-permute-done.6 = bf16[256,2,128]{2,1,0:T(2,128)(2,1)S(1)} collective-permute-done((bf16[256,2,128]{2,1,0:T(2,128)(2,1)S(1)}, bf16[256,2,128]{2,1,0:T(2,128)(2,1)S(1)}, u32[]{:S(2)}, u32[]{:S(2)}) %collective-permute-start.6) | collective-permute-done | bytes 131104 | tf_op jit(solution)/shard_map/ppermute | solution.py:300
  14.1 0.1 collective-permute-start.7
  14.2 0.0 copy-start
  14.2 0.7 %copy-done = s32[768]{0:T(1024)S(1)} copy-done((s32[768]{0:T(1024)S(1)}, s32[768]{0:T(1024)}, u32[]{:S(2)}) %copy-start) | copy-done | bytes 3096
  14.9 1.3 %prepare.1 = (bf16[2048,128]{1,0:T(8,128)(2,1)S(1)}, bf16[2,256,768]{2,1,0:T(8,128)(2,1)S(1)}, bf16[512,128]{1,0:T(8,128)(2,1)S(1)}) custom-call(s32[768]{0:T(1024)S(1)} %copy-done, bf16[96,16,128]{2,1,0:T(8,128)(2,1)} %query_hbm.1, bf16[512,128]{1,0:T(8,128)(2,1)} %bitcast.19), custom_call_target="tpu_custom_call" | custom-call | tf_op jit(solution)/shard_map/prepare/pallas_call | solution.py:331
  16.2 1.1 %shard_map.37 = (f32[512,1536]{1,0:T(8,128)S(1)}, f32[1,1536]{1,0:T(1,128)S(1)}, f32[1,1536]{1,0:T(1,128)S(1)}) custom-call(bf16[2048,128]{1,0:T(8,128)(2,1)S(1)} %get-tuple-element.20.mask_ref, bf16[2,256,768]{2,1,0:T(8,128)(2,1)S(1)} %get-tuple-element.21.turned_ref, bf16[512,128]{1,0:T(8,128)(2,1)S(1)} %get-tuple-element.22.refs_0_, ...), custom_call_target="tpu_custom_call" | custom-call | tf_op jit(solution)/shard_map/pallas_call | solution.py:356
  17.3 0.6 %shard_map.40 = (f32[256,1536]{1,0:T(8,128)S(1)}, f32[1,1536]{1,0:T(1,128)S(1)}, f32[1,1536]{1,0:T(1,128)S(1)}) custom-call(bf16[2048,128]{1,0:T(8,128)(2,1)S(1)} %get-tuple-element.20.mask_ref, bf16[2,256,768]{2,1,0:T(8,128)(2,1)S(1)} %get-tuple-element.21.turned_ref, bf16[512,128]{1,0:T(8,128)(2,1)S(1)} %pick.1.refs_0_), custom_call_target="tpu_custom_call" | custom-call | tf_op jit(solution)/shard_map/pallas_call | solution.py:356
  17.9 0.0 collective-permute-done.2
  17.9 1.1 %shard_map.38 = (f32[512,1536]{1,0:T(8,128)S(1)}, f32[1,1536]{1,0:T(1,128)S(1)}, f32[1,1536]{1,0:T(1,128)S(1)}) custom-call(bf16[2048,128]{1,0:T(8,128)(2,1)S(1)} %get-tuple-element.20.mask_ref, bf16[2,256,768]{2,1,0:T(8,128)(2,1)S(1)} %get-tuple-element.21.turned_ref, bf16[512,128]{1,0:T(8,128)(2,1)S(1)} %bitcast.13, bf16[512,128]{1,0:T(8,128)(2,1)S(1)} %bitcast.15), custom_call_target="tpu_custom_call" | custom-call | tf_op jit(solution)/shard_map/pallas_call | solution.py:356
  19.0 0.0 collective-permute-done.4
  19.0 1.1 %shard_map.39 = (f32[512,1536]{1,0:T(8,128)S(1)}, f32[1,1536]{1,0:T(1,128)S(1)}, f32[1,1536]{1,0:T(1,128)S(1)}) custom-call(bf16[2048,128]{1,0:T(8,128)(2,1)S(1)} %get-tuple-element.20.mask_ref, bf16[2,256,768]{2,1,0:T(8,128)(2,1)S(1)} %get-tuple-element.21.turned_ref, bf16[512,128]{1,0:T(8,128)(2,1)S(1)} %bitcast.12, bf16[512,128]{1,0:T(8,128)(2,1)S(1)} %bitcast.14), custom_call_target="tpu_custom_call" | custom-call | tf_op jit(solution)/shard_map/pallas_call | solution.py:356
  20.1 0.0 collective-permute-done.7
  20.1 1.7 %columns.1 = f32[32,1,256]{2,1,0:T(1,128)S(1)} custom-call(bf16[2048,128]{1,0:T(8,128)(2,1)S(1)} %get-tuple-element.20.mask_ref, bf16[2,256,768]{2,1,0:T(8,128)(2,1)S(1)} %get-tuple-element.21.turned_ref, f32[512,1536]{1,0:T(8,128)S(1)} %get-tuple-element.23.refs_0_, f32[1,1536]{1,0:T(1,128)S(1)} %get-tuple-element.24.refs_1_, ...), custom_call_target="tpu_custom_call" | custom-call | tf_op jit(solution)/shard_map/columns/pallas_call | solution.py:374
  21.8 12.1 %all_to_all.5 = f32[32,1,256]{2,1,0:T(1,128)S(1)} all-to-all(f32[32,1,256]{2,1,0:T(1,128)S(1)} %columns.1), channel_id=1, replica_groups=mesh['kv'=4,'seq'=8] {'kv','seq'}, dimensions={0} | all-to-all | bytes 65536 | tf_op jit(solution)/shard_map/all_to_all | solution.py:388
  33.9 0.6 %reduce_sum.9 = f32[256]{0:T(256)} reduce(f32[32,1,256]{2,1,0:T(1,128)S(1)} %all_to_all.5, f32[]{:T(128)} %constant.0.clone.1), dimensions={0,1}, to_apply=%region_0.0 | reduce | flops 7936 | bytes 33796 | tf_op jit(solution)/shard_map/reduce_sum | solution.py:389
  (3 shorter events, 0.0 us)
Async XLA Ops:
  0.0 8.3 %collective-permute-start.1 = (bf16[256,2,128]{2,1,0:T(2,128)(2,1)}, bf16[256,2,128]{2,1,0:T(2,128)(2,1)S(1)}, u32[]{:S(2)}, u32[]{:S(2)}) collective-permute-start(bf16[256,2,128]{2,1,0:T(2,128)(2,1)} %param.5), channel_id=1, source_target_pairs={{0,4},{1,5},{2,0},{3,1},{4,6},{5,7},{6,2},{7,3},{8,12},{9,13},{10,... | collective-permute-start | bytes 393224 | tf_op jit(solution)/shard_map/ppermute | solution.py:295
  4.1 8.1 %collective-permute-start.3 = (bf16[256,2,128]{2,1,0:T(2,128)(2,1)}, bf16[256,2,128]{2,1,0:T(2,128)(2,1)S(1)}, u32[]{:S(2)}, u32[]{:S(2)}) collective-permute-start(bf16[256,2,128]{2,1,0:T(2,128)(2,1)} %param.5), channel_id=1, source_target_pairs={{0,2},{1,3},{2,6},{3,7},{4,0},{5,1},{6,4},{7,5},{8,10},{9,11},{10,... | collective-permute-start | bytes 393224 | tf_op jit(solution)/shard_map/ppermute | solution.py:296
  4.1 8.1 %collective-permute-start.5 = (bf16[256,2,128]{2,1,0:T(2,128)(2,1)}, bf16[256,2,128]{2,1,0:T(2,128)(2,1)S(1)}, u32[]{:S(2)}, u32[]{:S(2)}) collective-permute-start(bf16[256,2,128]{2,1,0:T(2,128)(2,1)} %param.5), channel_id=1, source_target_pairs={{0,1},{1,0},{2,4},{3,5},{4,2},{5,3},{6,7},{7,6},{8,9},{9,8},{10,12... | collective-permute-start | bytes 393224 | tf_op jit(solution)/shard_map/ppermute | solution.py:299
  8.3 5.8 %collective-permute-start.6 = (bf16[256,2,128]{2,1,0:T(2,128)(2,1)S(1)}, bf16[256,2,128]{2,1,0:T(2,128)(2,1)S(1)}, u32[]{:S(2)}, u32[]{:S(2)}) collective-permute-start(bf16[256,2,128]{2,1,0:T(2,128)(2,1)S(1)} %collective-permute-done.1), channel_id=1, source_target_pairs={{0,2},{1,3},{2,0},{3,1},{4,6},{5,7},{6,4},{7,5},{8,10},{9,11},{10,... | collective-permute-start | bytes 393224 | tf_op jit(solution)/shard_map/ppermute | solution.py:300
  10.5 5.7 %collective-permute-start = (bf16[256,2,128]{2,1,0:T(2,128)(2,1)}, bf16[256,2,128]{2,1,0:T(2,128)(2,1)S(1)}, u32[]{:S(2)}, u32[]{:S(2)}) collective-permute-start(bf16[256,2,128]{2,1,0:T(2,128)(2,1)} %param.5), channel_id=1, source_target_pairs={{0,1},{1,0},{2,3},{3,2},{4,5},{5,4},{6,7},{7,6},{8,9},{9,8},{10,11... | collective-permute-start | bytes 393224 | tf_op jit(solution)/shard_map/ppermute | solution.py:312
  10.5 7.4 %collective-permute-start.2 = (bf16[256,2,128]{2,1,0:T(2,128)(2,1)S(1)}, bf16[256,2,128]{2,1,0:T(2,128)(2,1)S(1)}, u32[]{:S(2)}, u32[]{:S(2)}) collective-permute-start(bf16[256,2,128]{2,1,0:T(2,128)(2,1)S(1)} %collective-permute-done.1), channel_id=1, source_target_pairs={{0,1},{1,0},{2,3},{3,2},{4,5},{5,4},{6,7},{7,6},{8,9},{9,8},{10,11... | collective-permute-start | bytes 393224 | tf_op jit(solution)/shard_map/ppermute | solution.py:312
  12.2 6.8 %collective-permute-start.4 = (bf16[256,2,128]{2,1,0:T(2,128)(2,1)S(1)}, bf16[256,2,128]{2,1,0:T(2,128)(2,1)S(1)}, u32[]{:S(2)}, u32[]{:S(2)}) collective-permute-start(bf16[256,2,128]{2,1,0:T(2,128)(2,1)S(1)} %collective-permute-done.3), channel_id=1, source_target_pairs={{0,1},{1,0},{2,3},{3,2},{4,5},{5,4},{6,7},{7,6},{8,9},{9,8},{10,11... | collective-permute-start | bytes 393224 | tf_op jit(solution)/shard_map/ppermute | solution.py:312
  14.1 6.0 %collective-permute-start.7 = (bf16[256,2,128]{2,1,0:T(2,128)(2,1)S(1)}, bf16[256,2,128]{2,1,0:T(2,128)(2,1)S(1)}, u32[]{:S(2)}, u32[]{:S(2)}) collective-permute-start(bf16[256,2,128]{2,1,0:T(2,128)(2,1)S(1)} %bitcast.10), channel_id=1, source_target_pairs={{0,1},{1,0},{2,3},{3,2},{4,5},{5,4},{6,7},{7,6},{8,9},{9,8},{10,11... | collective-permute-start | bytes 393224 | tf_op jit(solution)/shard_map/ppermute | solution.py:312
  14.2 0.7 %copy-start = (s32[768]{0:T(1024)S(1)}, s32[768]{0:T(1024)}, u32[]{:S(2)}) copy-start(s32[768]{0:T(1024)} %row_ref.1) | copy-start | bytes 9220

commit v6 on v5

--- a/solution.py
+++ b/solution.py
@@ -266,6 +266,10 @@
 
 def ring_of(chips):
     return list(range(0, chips, 2)) + list(range(1, chips, 2))[::-1]
+
+
+def add_kernel(received_ref, out_ref):
+    out_ref[...] = jnp.sum(received_ref[...], axis=(0, 1))
 
 
 def pick_kernel(ends, near_ref, far_ref, out_ref):
@@ -386,7 +390,14 @@
         name="columns",
     )(mask, turned, *stages, *blocks)
     received = lax.all_to_all(partial, ("kv", "seq"), 0, 0, tiled=True)
-    return jnp.sum(received, axis=(0, 1))
+    return pl.pallas_call(
+        add_kernel,
+        out_shape=jax.ShapeDtypeStruct((local_keys,), jnp.float32),
+        in_specs=[WHOLE],
+        out_specs=WHOLE,
+        compiler_params=grant(4 if amount <= SPAN else 32),
+        name="add",
+    )(received)
 
 
 def solution(mesh):

time: 34.7 us -> 34.7 us (level)
  other arithmetic: 0.62 us -> 0 us
  Pallas kernels: 6.86 us -> 7.46 us
    reduce_sum x1 -> x0, other arithmetic: 0.62 us -> none  [on_device(): return jnp.sum(received, axis=(0, 1))]
    pallas_call x0 -> x1, Pallas kernels: none -> 0.61 us  [on_device(): pl.pallas_call(add_kernel, out_shape=jax.ShapeDtypeStruct((local_keys,),...]
where the time goes in v6:
time: 34.7 us; the launch traced here: 34.5 us
  blocking collectives  12.1 us (35%)
  Pallas kernels  7.46 us (21%)
  waiting for transfers between devices  7.25 us (21%)
  starting transfers between devices  6.91 us (20%)
  local copies, waits for them, and re-layouts  0.68 us (2%)
    all_to_all x1, blocking collectives, on_device(): received = lax.all_to_all(partial, ('kv', 'seq'), 0, 0, tiled=True)  12.1 us
    ppermute x1, waiting for transfers between devices, gather_keys(): blocks['left'] = lax.ppermute(key_vectors, 'seq', ahead)  4.2 us
    ppermute x1, starting transfers between devices, gather_keys(): blocks['left'] = lax.ppermute(key_vectors, 'seq', ahead)  4.06 us
    pallas_call x4, Pallas kernels, on_device(): pl.pallas_call(functools.partial(stage_kernel, first * local_keys), out_s...  3.9 us
    ppermute x1, starting transfers between devices, gather_keys(): far = lax.ppermute(blocks['left'], 'seq', [(i, i ^ 2) for i in range(size)])  2.26 us
    ppermute x1, waiting for transfers between devices, gather_keys(): far = lax.ppermute(blocks['left'], 'seq', [(i, i ^ 2) for i in range(size)])  1.87 us
    pallas_call x1, Pallas kernels, on_device(): pl.pallas_call(functools.partial(column_kernel, owners, counts, others, l...  1.65 us
    pallas_call x1, Pallas kernels, on_device(): pl.pallas_call(functools.partial(prepare_kernel, members, owners), out_sh...  1.3 us
  transfers between devices with their start and end apart: 8, of which 3 were waited for; matrix products, arithmetic and copies ran while one was open for 0% of the time, Pallas kernels for 15%

profile of v6, /device:TPU:0, one launch (start us, length us, event | category | flops | bytes accessed | tf_op | source)
XLA Modules:
  0.0 34.5 jit_solution(14013935805250447997)
XLA Ops:
  0.0 4.1 %collective-permute-start.1 = (bf16[256,2,128]{2,1,0:T(2,128)(2,1)}, bf16[256,2,128]{2,1,0:T(2,128)(2,1)S(1)}, u32[]{:S(2)}, u32[]{:S(2)}) collective-permute-start(bf16[256,2,128]{2,1,0:T(2,128)(2,1)} %param.5), channel_id=1, source_target_pairs={{0,4},{1,5},{2,0},{3,1},{4,6},{5,7},{6,2},{7,3},{8,12},{9,13},{10,... | collective-permute-start | bytes 393224 | tf_op jit(solution)/shard_map/ppermute | solution.py:299
  4.1 0.0 collective-permute-start.3
  4.1 0.0 collective-permute-start.5
  4.1 4.2 %collective-permute-done.1 = bf16[256,2,128]{2,1,0:T(2,128)(2,1)S(1)} collective-permute-done((bf16[256,2,128]{2,1,0:T(2,128)(2,1)}, bf16[256,2,128]{2,1,0:T(2,128)(2,1)S(1)}, u32[]{:S(2)}, u32[]{:S(2)}) %collective-permute-start.1) | collective-permute-done | bytes 131104 | tf_op jit(solution)/shard_map/ppermute | solution.py:299
  8.3 2.3 %collective-permute-start.6 = (bf16[256,2,128]{2,1,0:T(2,128)(2,1)S(1)}, bf16[256,2,128]{2,1,0:T(2,128)(2,1)S(1)}, u32[]{:S(2)}, u32[]{:S(2)}) collective-permute-start(bf16[256,2,128]{2,1,0:T(2,128)(2,1)S(1)} %collective-permute-done.1), channel_id=1, source_target_pairs={{0,2},{1,3},{2,0},{3,1},{4,6},{5,7},{6,4},{7,5},{8,10},{9,11},{10,... | collective-permute-start | bytes 393224 | tf_op jit(solution)/shard_map/ppermute | solution.py:304
  10.5 0.0 collective-permute-start
  10.5 0.5 %collective-permute-start.2 = (bf16[256,2,128]{2,1,0:T(2,128)(2,1)S(1)}, bf16[256,2,128]{2,1,0:T(2,128)(2,1)S(1)}, u32[]{:S(2)}, u32[]{:S(2)}) collective-permute-start(bf16[256,2,128]{2,1,0:T(2,128)(2,1)S(1)} %collective-permute-done.1), channel_id=1, source_target_pairs={{0,1},{1,0},{2,3},{3,2},{4,5},{5,4},{6,7},{7,6},{8,9},{9,8},{10,11... | collective-permute-start | bytes 393224 | tf_op jit(solution)/shard_map/ppermute | solution.py:316
  11.0 1.2 %collective-permute-done.3 = bf16[256,2,128]{2,1,0:T(2,128)(2,1)S(1)} collective-permute-done((bf16[256,2,128]{2,1,0:T(2,128)(2,1)}, bf16[256,2,128]{2,1,0:T(2,128)(2,1)S(1)}, u32[]{:S(2)}, u32[]{:S(2)}) %collective-permute-start.3) | collective-permute-done | bytes 131104 | tf_op jit(solution)/shard_map/ppermute | solution.py:300
  12.2 0.0 collective-permute-start.4
  12.2 1.9 %collective-permute-done.6 = bf16[256,2,128]{2,1,0:T(2,128)(2,1)S(1)} collective-permute-done((bf16[256,2,128]{2,1,0:T(2,128)(2,1)S(1)}, bf16[256,2,128]{2,1,0:T(2,128)(2,1)S(1)}, u32[]{:S(2)}, u32[]{:S(2)}) %collective-permute-start.6) | collective-permute-done | bytes 131104 | tf_op jit(solution)/shard_map/ppermute | solution.py:304
  14.1 0.1 collective-permute-start.7
  14.2 0.0 copy-start
  14.2 0.7 %copy-done = s32[768]{0:T(1024)S(1)} copy-done((s32[768]{0:T(1024)S(1)}, s32[768]{0:T(1024)}, u32[]{:S(2)}) %copy-start) | copy-done | bytes 3096
  14.9 1.3 %prepare.1 = (bf16[2048,128]{1,0:T(8,128)(2,1)S(1)}, bf16[2,256,768]{2,1,0:T(8,128)(2,1)S(1)}, bf16[512,128]{1,0:T(8,128)(2,1)S(1)}) custom-call(s32[768]{0:T(1024)S(1)} %copy-done, bf16[96,16,128]{2,1,0:T(8,128)(2,1)} %query_hbm.1, bf16[512,128]{1,0:T(8,128)(2,1)} %bitcast.19), custom_call_target="tpu_custom_call" | custom-call | tf_op jit(solution)/shard_map/prepare/pallas_call | solution.py:335
  16.2 1.1 %shard_map.37 = (f32[512,1536]{1,0:T(8,128)S(1)}, f32[1,1536]{1,0:T(1,128)S(1)}, f32[1,1536]{1,0:T(1,128)S(1)}) custom-call(bf16[2048,128]{1,0:T(8,128)(2,1)S(1)} %get-tuple-element.20.mask_ref, bf16[2,256,768]{2,1,0:T(8,128)(2,1)S(1)} %get-tuple-element.21.turned_ref, bf16[512,128]{1,0:T(8,128)(2,1)S(1)} %get-tuple-element.22.refs_0_, ...), custom_call_target="tpu_custom_call" | custom-call | tf_op jit(solution)/shard_map/pallas_call | solution.py:360
  17.3 0.6 %shard_map.40 = (f32[256,1536]{1,0:T(8,128)S(1)}, f32[1,1536]{1,0:T(1,128)S(1)}, f32[1,1536]{1,0:T(1,128)S(1)}) custom-call(bf16[2048,128]{1,0:T(8,128)(2,1)S(1)} %get-tuple-element.20.mask_ref, bf16[2,256,768]{2,1,0:T(8,128)(2,1)S(1)} %get-tuple-element.21.turned_ref, bf16[512,128]{1,0:T(8,128)(2,1)S(1)} %pick.1.refs_0_), custom_call_target="tpu_custom_call" | custom-call | tf_op jit(solution)/shard_map/pallas_call | solution.py:360
  17.9 0.0 collective-permute-done.2
  17.9 1.1 %shard_map.38 = (f32[512,1536]{1,0:T(8,128)S(1)}, f32[1,1536]{1,0:T(1,128)S(1)}, f32[1,1536]{1,0:T(1,128)S(1)}) custom-call(bf16[2048,128]{1,0:T(8,128)(2,1)S(1)} %get-tuple-element.20.mask_ref, bf16[2,256,768]{2,1,0:T(8,128)(2,1)S(1)} %get-tuple-element.21.turned_ref, bf16[512,128]{1,0:T(8,128)(2,1)S(1)} %bitcast.13, bf16[512,128]{1,0:T(8,128)(2,1)S(1)} %bitcast.15), custom_call_target="tpu_custom_call" | custom-call | tf_op jit(solution)/shard_map/pallas_call | solution.py:360
  19.0 0.0 collective-permute-done.4
  19.0 1.1 %shard_map.39 = (f32[512,1536]{1,0:T(8,128)S(1)}, f32[1,1536]{1,0:T(1,128)S(1)}, f32[1,1536]{1,0:T(1,128)S(1)}) custom-call(bf16[2048,128]{1,0:T(8,128)(2,1)S(1)} %get-tuple-element.20.mask_ref, bf16[2,256,768]{2,1,0:T(8,128)(2,1)S(1)} %get-tuple-element.21.turned_ref, bf16[512,128]{1,0:T(8,128)(2,1)S(1)} %bitcast.12, bf16[512,128]{1,0:T(8,128)(2,1)S(1)} %bitcast.14), custom_call_target="tpu_custom_call" | custom-call | tf_op jit(solution)/shard_map/pallas_call | solution.py:360
  20.1 0.0 collective-permute-done.7
  20.1 1.7 %columns.1 = f32[32,1,256]{2,1,0:T(1,128)S(1)} custom-call(bf16[2048,128]{1,0:T(8,128)(2,1)S(1)} %get-tuple-element.20.mask_ref, bf16[2,256,768]{2,1,0:T(8,128)(2,1)S(1)} %get-tuple-element.21.turned_ref, f32[512,1536]{1,0:T(8,128)S(1)} %get-tuple-element.23.refs_0_, f32[1,1536]{1,0:T(1,128)S(1)} %get-tuple-element.24.refs_1_, ...), custom_call_target="tpu_custom_call" | custom-call | tf_op jit(solution)/shard_map/columns/pallas_call | solution.py:378
  21.8 12.1 %all_to_all.5.received_ref = f32[32,1,256]{2,1,0:T(1,128)S(1)} all-to-all(f32[32,1,256]{2,1,0:T(1,128)S(1)} %columns.1), channel_id=1, replica_groups=mesh['kv'=4,'seq'=8] {'kv','seq'}, dimensions={0} | all-to-all | bytes 65536 | tf_op jit(solution)/shard_map/all_to_all | solution.py:392
  33.9 0.6 %add.1 = f32[256]{0:T(256)} custom-call(f32[32,1,256]{2,1,0:T(1,128)S(1)} %all_to_all.5.received_ref), custom_call_target="tpu_custom_call" | custom-call | tf_op jit(solution)/shard_map/add/pallas_call | solution.py:393
  (3 shorter events, 0.0 us)
Async XLA Ops:
  0.0 8.3 %collective-permute-start.1 = (bf16[256,2,128]{2,1,0:T(2,128)(2,1)}, bf16[256,2,128]{2,1,0:T(2,128)(2,1)S(1)}, u32[]{:S(2)}, u32[]{:S(2)}) collective-permute-start(bf16[256,2,128]{2,1,0:T(2,128)(2,1)} %param.5), channel_id=1, source_target_pairs={{0,4},{1,5},{2,0},{3,1},{4,6},{5,7},{6,2},{7,3},{8,12},{9,13},{10,... | collective-permute-start | bytes 393224 | tf_op jit(solution)/shard_map/ppermute | solution.py:299
  4.1 8.1 %collective-permute-start.3 = (bf16[256,2,128]{2,1,0:T(2,128)(2,1)}, bf16[256,2,128]{2,1,0:T(2,128)(2,1)S(1)}, u32[]{:S(2)}, u32[]{:S(2)}) collective-permute-start(bf16[256,2,128]{2,1,0:T(2,128)(2,1)} %param.5), channel_id=1, source_target_pairs={{0,2},{1,3},{2,6},{3,7},{4,0},{5,1},{6,4},{7,5},{8,10},{9,11},{10,... | collective-permute-start | bytes 393224 | tf_op jit(solution)/shard_map/ppermute | solution.py:300
  4.1 8.1 %collective-permute-start.5 = (bf16[256,2,128]{2,1,0:T(2,128)(2,1)}, bf16[256,2,128]{2,1,0:T(2,128)(2,1)S(1)}, u32[]{:S(2)}, u32[]{:S(2)}) collective-permute-start(bf16[256,2,128]{2,1,0:T(2,128)(2,1)} %param.5), channel_id=1, source_target_pairs={{0,1},{1,0},{2,4},{3,5},{4,2},{5,3},{6,7},{7,6},{8,9},{9,8},{10,12... | collective-permute-start | bytes 393224 | tf_op jit(solution)/shard_map/ppermute | solution.py:303
  8.3 5.8 %collective-permute-start.6 = (bf16[256,2,128]{2,1,0:T(2,128)(2,1)S(1)}, bf16[256,2,128]{2,1,0:T(2,128)(2,1)S(1)}, u32[]{:S(2)}, u32[]{:S(2)}) collective-permute-start(bf16[256,2,128]{2,1,0:T(2,128)(2,1)S(1)} %collective-permute-done.1), channel_id=1, source_target_pairs={{0,2},{1,3},{2,0},{3,1},{4,6},{5,7},{6,4},{7,5},{8,10},{9,11},{10,... | collective-permute-start | bytes 393224 | tf_op jit(solution)/shard_map/ppermute | solution.py:304
  10.5 5.7 %collective-permute-start = (bf16[256,2,128]{2,1,0:T(2,128)(2,1)}, bf16[256,2,128]{2,1,0:T(2,128)(2,1)S(1)}, u32[]{:S(2)}, u32[]{:S(2)}) collective-permute-start(bf16[256,2,128]{2,1,0:T(2,128)(2,1)} %param.5), channel_id=1, source_target_pairs={{0,1},{1,0},{2,3},{3,2},{4,5},{5,4},{6,7},{7,6},{8,9},{9,8},{10,11... | collective-permute-start | bytes 393224 | tf_op jit(solution)/shard_map/ppermute | solution.py:316
  10.5 7.4 %collective-permute-start.2 = (bf16[256,2,128]{2,1,0:T(2,128)(2,1)S(1)}, bf16[256,2,128]{2,1,0:T(2,128)(2,1)S(1)}, u32[]{:S(2)}, u32[]{:S(2)}) collective-permute-start(bf16[256,2,128]{2,1,0:T(2,128)(2,1)S(1)} %collective-permute-done.1), channel_id=1, source_target_pairs={{0,1},{1,0},{2,3},{3,2},{4,5},{5,4},{6,7},{7,6},{8,9},{9,8},{10,11... | collective-permute-start | bytes 393224 | tf_op jit(solution)/shard_map/ppermute | solution.py:316
  12.2 6.8 %collective-permute-start.4 = (bf16[256,2,128]{2,1,0:T(2,128)(2,1)S(1)}, bf16[256,2,128]{2,1,0:T(2,128)(2,1)S(1)}, u32[]{:S(2)}, u32[]{:S(2)}) collective-permute-start(bf16[256,2,128]{2,1,0:T(2,128)(2,1)S(1)} %collective-permute-done.3), channel_id=1, source_target_pairs={{0,1},{1,0},{2,3},{3,2},{4,5},{5,4},{6,7},{7,6},{8,9},{9,8},{10,11... | collective-permute-start | bytes 393224 | tf_op jit(solution)/shard_map/ppermute | solution.py:316
  14.1 6.0 %collective-permute-start.7 = (bf16[256,2,128]{2,1,0:T(2,128)(2,1)S(1)}, bf16[256,2,128]{2,1,0:T(2,128)(2,1)S(1)}, u32[]{:S(2)}, u32[]{:S(2)}) collective-permute-start(bf16[256,2,128]{2,1,0:T(2,128)(2,1)S(1)} %bitcast.10), channel_id=1, source_target_pairs={{0,1},{1,0},{2,3},{3,2},{4,5},{5,4},{6,7},{7,6},{8,9},{9,8},{10,11... | collective-permute-start | bytes 393224 | tf_op jit(solution)/shard_map/ppermute | solution.py:316
  14.2 0.7 %copy-start = (s32[768]{0:T(1024)S(1)}, s32[768]{0:T(1024)}, u32[]{:S(2)}) copy-start(s32[768]{0:T(1024)} %row_ref.1) | copy-start | bytes 9220
